TPU v7x, 256 devices: a whole 4x4x8 slice. The times are simulated.
256 devices in a mesh: dp: 16 (over y, x), expert: 16 (over z, core).
Axes of the slice: x: 4, y: 4, z: 8, core: 2. Of those that a mesh axis runs over, the one named last changes fastest.
Arguments:
- tokens: bfloat16 [65536, 1024], P(('dp', 'expert')), may hold values from -24 to 24
- cotangent: bfloat16 [65536, 1024], P(('dp', 'expert')), may hold values from -6 to 6
- gates: bfloat16 [65536, 2], P(('dp', 'expert')), may hold values from 0.099609375 to 1
- expert_ids: int32 [65536, 2], P(('dp', 'expert')), may hold values from 0 to 15, all different within a row; in each aligned block of 128 rows (0 to 127, 128 to 255, ...) at most 32 rows name the same one
- expert_weights: bfloat16 [16, 3, 1024, 768], P('expert'), may hold values from -0.1875 to 0.1875
Outputs:
- tokens_grad: bfloat16 [65536, 1024], P(('dp', 'expert'))
- gates_grad: bfloat16 [65536, 2], P(('dp', 'expert'))
- weights_grad: bfloat16 [16, 3, 1024, 768], P('expert', None, 'dp')
Inputs may be any that keep to these rules, and one draw needn't show every extreme that they name: `expert_ids`: within each micro-batch of 128 tokens of one device no expert is named by more than 32 routes, a bound that some block reaches; the two ids of a token differ.
All inputs are finite; a program needn't handle non-finite values.
Results may differ from a plain program's by a relative error of at most 0.017.
Values may be sent and summed in bfloat16 or wider, within the bound.
A program may use at most 64 MiB of HBM per device.

v0:
```python
import jax
import jax.numpy as jnp
from jax import lax
from jax.sharding import PartitionSpec as P

MICRO = 2
PAD = 128

F32 = jnp.float32
BF16 = jnp.bfloat16

CONTRACT_LAST = (((1,), (1,)), ((), ()))
CONTRACT_FIRST = (((0,), (0,)), ((), ()))


def mm(a, b):
    return jnp.dot(a, b, preferred_element_type=F32)


def route_masks(ids_block, expert_count, capacity):
    flat_ids = ids_block.reshape(-1)
    one_hot = (flat_ids[:, None] == jnp.arange(expert_count, dtype=jnp.int32)[None, :]).astype(
        jnp.int32
    )
    earlier = jnp.cumsum(one_hot, axis=0) - one_hot
    rank_slot = jnp.sum(earlier * one_hot, axis=1)
    route_slot = (flat_ids * capacity + rank_slot).reshape(-1, 2)
    position = jnp.arange(expert_count * capacity, dtype=jnp.int32)[:, None]
    return position == route_slot[None, :, 0], position == route_slot[None, :, 1]


def expert_step(recv, w_gate, w_up, w_down, width):
    rows_in = recv[:, :width]
    scaled = recv[:, width:]
    pre_gate = mm(rows_in, w_gate)
    pre_up = mm(rows_in, w_up)
    sigmoid_gate = jax.nn.sigmoid(pre_gate)
    activated = pre_gate * sigmoid_gate
    hidden = (activated * pre_up).astype(BF16)
    hidden_grad = mm(scaled, w_down)
    gate_sum = jnp.sum(hidden.astype(F32) * hidden_grad, axis=1)
    grad_pre_gate = (
        hidden_grad * pre_up * sigmoid_gate * (1.0 + pre_gate * (1.0 - sigmoid_gate))
    ).astype(BF16)
    grad_pre_up = (hidden_grad * activated).astype(BF16)
    input_grad = (
        lax.dot_general(grad_pre_gate, w_gate, CONTRACT_LAST, preferred_element_type=F32)
        + lax.dot_general(grad_pre_up, w_up, CONTRACT_LAST, preferred_element_type=F32)
    ).astype(BF16)
    grads = (
        lax.dot_general(rows_in, grad_pre_gate, CONTRACT_FIRST, preferred_element_type=F32),
        lax.dot_general(rows_in, grad_pre_up, CONTRACT_FIRST, preferred_element_type=F32),
        lax.dot_general(scaled, hidden, CONTRACT_FIRST, preferred_element_type=F32),
    )
    high = gate_sum.astype(BF16)
    low = (gate_sum - high.astype(F32)).astype(BF16)
    tail = jnp.concatenate(
        [high[:, None], low[:, None], jnp.zeros((recv.shape[0], PAD - 2), BF16)], axis=1
    )
    return jnp.concatenate([input_grad, tail], axis=1), grads


def on_device(tokens, cotangent, gates, expert_ids, expert_weights):
    n_expert = lax.axis_size("expert")
    expert_count = n_expert * expert_weights.shape[0]
    batch_rows = tokens.shape[0] // MICRO
    capacity = max(2, 4 * batch_rows // expert_count)
    width = tokens.shape[1]
    w_gate, w_up, w_down = expert_weights[0, 0], expert_weights[0, 1], expert_weights[0, 2]

    token_parts, gate_parts = [], []
    totals = None
    for micro_index in range(MICRO):
        lower = micro_index * batch_rows
        upper = lower + batch_rows
        first, second = route_masks(expert_ids[lower:upper], expert_count, capacity)
        both = (first | second).astype(BF16)
        cot = cotangent[lower:upper].astype(F32)
        gate = gates[lower:upper].astype(F32)
        scaled_first = (gate[:, 0:1] * cot).astype(BF16)
        scaled_second = (gate[:, 1:2] * cot).astype(BF16)
        rows_in = mm(both, tokens[lower:upper]).astype(BF16)
        rows_scaled = (
            mm(first.astype(BF16), scaled_first) + mm(second.astype(BF16), scaled_second)
        ).astype(BF16)
        payload = jnp.concatenate([rows_in, rows_scaled], axis=1).reshape(
            n_expert, -1, 2 * width
        )
        recv = lax.all_to_all(payload, "expert", 0, 0, tiled=True).reshape(-1, 2 * width)
        back, grads = expert_step(recv, w_gate, w_up, w_down, width)
        totals = grads if totals is None else tuple(t + g for t, g in zip(totals, grads))
        ret = lax.all_to_all(
            back.reshape(n_expert, -1, width + PAD), "expert", 0, 0, tiled=True
        ).reshape(-1, width + PAD)
        token_grad = lax.dot_general(
            both, ret[:, :width], CONTRACT_FIRST, preferred_element_type=F32
        ).astype(BF16)
        gate_sum = ret[:, width].astype(F32) + ret[:, width + 1].astype(F32)
        sum_first = jnp.sum(jnp.where(first, gate_sum[:, None], 0.0), axis=0)
        sum_second = jnp.sum(jnp.where(second, gate_sum[:, None], 0.0), axis=0)
        gate_grad = jnp.stack([sum_first / gate[:, 0], sum_second / gate[:, 1]], axis=1)
        token_parts.append(token_grad)
        gate_parts.append(gate_grad.astype(BF16))

    rounded = jnp.stack(totals).astype(BF16)[None]
    weights_grad = lax.psum_scatter(rounded, "dp", scatter_dimension=2, tiled=True)
    return (
        jnp.concatenate(token_parts, axis=0),
        jnp.concatenate(gate_parts, axis=0),
        weights_grad,
    )


def solution(mesh):
    placed = (
        P(("dp", "expert"), None),
        P(("dp", "expert"), None),
        P(("dp", "expert"), None),
        P(("dp", "expert"), None),
        P("expert", None, None, None),
    )
    return jax.shard_map(
        on_device,
        mesh=mesh,
        in_specs=placed,
        out_specs=(
            P(("dp", "expert"), None),
            P(("dp", "expert"), None),
            P("expert", None, "dp", None),
        ),
        check_vma=False,
    )
```

profile of v0, /device:TPU:65, one launch (start us, length us, event | category | flops | bytes accessed | tf_op | source)
XLA Modules:
  0.0 236.1 jit_solution(4699976671651872209)
XLA Ops:
  10.3 1.4 convolution_convert_fusion
  12.7 1.5 pad_maximum_fusion.2
  14.2 8.6 %all-to-all-start.2 = ((bf16[16,32,2048]{2,1,0:T(8,128)(2,1)}), bf16[16,32,2048]{2,1,0:T(8,128)(2,1)S(1)}, u32[]{:S(2)}, u32[]{:S(2)}) async-start(bf16[16,32,2048]{2,1,0:T(8,128)(2,1)} %bitcast.125), calls=%async_computation.2 | async-start | bytes 4194304 | tf_op jit(solution)/shard_map/all_to_all | solution.py:89
  26.0 1.5 pad_maximum_fusion.1
  27.5 42.9 %all-to-all-done.2 = bf16[16,32,2048]{2,1,0:T(8,128)(2,1)S(1)} async-done(((bf16[16,32,2048]{2,1,0:T(8,128)(2,1)}), bf16[16,32,2048]{2,1,0:T(8,128)(2,1)S(1)}, u32[]{:S(2)}, u32[]{:S(2)}) %all-to-all-start.2) | async-done | bytes 2097184 | tf_op jit(solution)/shard_map/all_to_all | solution.py:89
  70.4 1.3 copy-done
  71.7 6.4 %all-to-all-start = ((bf16[16,32,2048]{2,1,0:T(8,128)(2,1)}), bf16[16,32,2048]{2,1,0:T(8,128)(2,1)S(1)}, u32[]{:S(2)}, u32[]{:S(2)}) async-start(bf16[16,32,2048]{2,1,0:T(8,128)(2,1)} %bitcast.126), calls=%async_computation | async-start | bytes 4194304 | tf_op jit(solution)/shard_map/all_to_all | solution.py:89
  78.3 4.0 %fusion.2 = f32[512,768]{1,0:T(8,128)} fusion(bf16[1,3,1024,768]{3,2,1,0:T(8,128)(2,1)} %param.9, bf16[512,2048]{1,0:T(8,128)(2,1)} %bitcast.119), kind=kOutput, calls=%fused_computation.12 | convolution fusion | flops 805306368 | bytes 4194304 | tf_op jit(solution)/shard_map/dot_general | solution.py:17
  82.4 3.6 %fusion.9 = f32[512,768]{1,0:T(8,128)} fusion(bf16[1,3,1024,768]{3,2,1,0:T(8,128)(2,1)} %param.9, bf16[512,2048]{1,0:T(8,128)(2,1)S(1)} %bitcast.120), kind=kOutput, calls=%fused_computation.19 | convolution fusion | flops 805306368 | bytes 4194304 | tf_op jit(solution)/shard_map/dot_general | solution.py:17
  86.0 39.7 %all-to-all-done = bf16[16,32,2048]{2,1,0:T(8,128)(2,1)S(1)} async-done(((bf16[16,32,2048]{2,1,0:T(8,128)(2,1)}), bf16[16,32,2048]{2,1,0:T(8,128)(2,1)S(1)}, u32[]{:S(2)}, u32[]{:S(2)}) %all-to-all-start) | async-done | bytes 2097184 | tf_op jit(solution)/shard_map/all_to_all | solution.py:89
  125.6 2.4 %fusion.6 = f32[512,768]{1,0:T(8,128)S(1)} fusion(bf16[1,3,1024,768]{3,2,1,0:T(8,128)(2,1)} %param.9, bf16[512,2048]{1,0:T(8,128)(2,1)S(1)} %bitcast.113), kind=kOutput, calls=%fused_computation.16 | convolution fusion | flops 805306368 | bytes 4194304 | tf_op jit(solution)/shard_map/dot_general | solution.py:17
  128.0 2.4 %fusion.12 = f32[512,768]{1,0:T(8,128)S(1)} fusion(bf16[1,3,1024,768]{3,2,1,0:T(8,128)(2,1)} %param.9, bf16[512,2048]{1,0:T(8,128)(2,1)S(1)} %bitcast.114), kind=kOutput, calls=%fused_computation.22 | convolution fusion | flops 805306368 | bytes 4194304 | tf_op jit(solution)/shard_map/dot_general | solution.py:17
  130.4 3.0 %multiply_reduce_fusion.1 = (f32[512]{0:T(512)S(1)}, bf16[512,768]{1,0:T(8,128)(2,1)S(1)}, bf16[512,768]{1,0:T(8,128)(2,1)S(1)}, bf16[512,768]{1,0:T(8,128)(2,1)S(1)}) fusion(f32[512,768]{1,0:T(8,128)S(1)} %fusion.12, f32[512,768]{1,0:T(8,128)S(1)} %fusion.6, bf16[1,3,1024,768]{3,2,1,0:T(8,128)(2,1)} %param.9, bf16[512,2048]{1,0:T(8,128)(2,1)S(1)} %bitcast.115), kind=kOutput, calls=%fused_computation.34 | convolution fusion | flops 812383744 | bytes 8128512 | tf_op jit(solution)/shard_map/dot_general | solution.py:17
  133.5 1.0 fusion.44
  134.7 1.0 fusion.46
  135.8 1.0 fusion.37
  138.2 3.0 %multiply_reduce_fusion = (f32[512]{0:T(512)S(1)}, bf16[512,768]{1,0:T(8,128)(2,1)S(1)}, bf16[512,768]{1,0:T(8,128)(2,1)S(1)}, bf16[512,768]{1,0:T(8,128)(2,1)S(1)}) fusion(f32[512,768]{1,0:T(8,128)S(1)} %copy-done.10, f32[512,768]{1,0:T(8,128)S(1)} %copy-done.9, bf16[1,3,1024,768]{3,2,1,0:T(8,128)(2,1)} %param.9, bf16[512,2048]{1,0:T(8,128)(2,1)S(1)} %bitcast.121), kind=kOutput, calls=%fused_computation.28 | convolution fusion | flops 812383744 | bytes 8128512 | tf_op jit(solution)/shard_map/dot_general | solution.py:17
  141.3 1.1 fusion.21
  142.4 1.1 fusion.20
  143.5 1.1 fusion.22
  144.6 2.6 %pad_maximum_fusion = bf16[1,3,1024,768]{3,2,1,0:T(8,128)(2,1)} fusion(bf16[1,1,1024,768]{3,2,1,0:T(8,128)(2,1)S(1)} %fusion.22, bf16[1,1,1024,768]{3,2,1,0:T(8,128)(2,1)S(1)} %fusion.21, bf16[1,1,1024,768]{3,2,1,0:T(8,128)(2,1)S(1)} %fusion.20), kind=kLoop, calls=%fused_computation | loop fusion | flops 4718592 | bytes 9437184 | tf_op jit(solution)/shard_map/stack | solution.py:105
  148.3 2.5 %fusion.4 = f32[512,1024]{1,0:T(8,128)S(1)} fusion(bf16[512,768]{1,0:T(8,128)(2,1)S(1)} %copy-done.7, bf16[1,3,1024,768]{3,2,1,0:T(8,128)(2,1)} %param.9), kind=kOutput, calls=%fused_computation.14 | convolution fusion | flops 805306368 | bytes 4456448 | tf_op jit(solution)/shard_map/dot_general | solution.py:47
  150.8 2.4 %add_convert_fusion.5 = bf16[512,1024]{1,0:T(8,128)(2,1)S(1)} fusion(f32[512,1024]{1,0:T(8,128)S(1)} %fusion.4, bf16[512,768]{1,0:T(8,128)(2,1)S(1)} %copy-done.5, bf16[1,3,1024,768]{3,2,1,0:T(8,128)(2,1)} %param.9), kind=kOutput, calls=%fused_computation.8 | convolution fusion | flops 806354944 | bytes 5505024 | tf_op jit(solution)/shard_map/dot_general | solution.py:48
  153.3 2.0 concatenate.37
  155.3 6.4 %all-to-all-start.1 = ((bf16[16,32,1152]{2,1,0:T(8,128)(2,1)}), bf16[16,32,1152]{2,1,0:T(8,128)(2,1)S(1)}, u32[]{:S(2)}, u32[]{:S(2)}) async-start(bf16[16,32,1152]{2,1,0:T(8,128)(2,1)} %concatenate.37), calls=%async_computation.1 | async-start | bytes 2359296 | tf_op jit(solution)/shard_map/all_to_all | solution.py:92
  162.2 2.4 %fusion = f32[512,1024]{1,0:T(8,128)S(1)} fusion(bf16[512,768]{1,0:T(8,128)(2,1)S(1)} %get-tuple-element.20, bf16[1,3,1024,768]{3,2,1,0:T(8,128)(2,1)} %param.9), kind=kOutput, calls=%fused_computation.10 | convolution fusion | flops 805306368 | bytes 4456448 | tf_op jit(solution)/shard_map/dot_general | solution.py:47
  164.7 2.5 %add_convert_fusion.3 = bf16[512,1024]{1,0:T(8,128)(2,1)S(1)} fusion(f32[512,1024]{1,0:T(8,128)S(1)} %fusion, bf16[512,768]{1,0:T(8,128)(2,1)S(1)} %get-tuple-element.22, bf16[1,3,1024,768]{3,2,1,0:T(8,128)(2,1)} %param.9), kind=kOutput, calls=%fused_computation.6 | convolution fusion | flops 806354944 | bytes 5505024 | tf_op jit(solution)/shard_map/dot_general | solution.py:48
  167.1 2.1 concatenate.40
  169.2 21.0 %all-to-all-done.1 = bf16[16,32,1152]{2,1,0:T(8,128)(2,1)S(1)} async-done(((bf16[16,32,1152]{2,1,0:T(8,128)(2,1)}), bf16[16,32,1152]{2,1,0:T(8,128)(2,1)S(1)}, u32[]{:S(2)}, u32[]{:S(2)}) %all-to-all-start.1) | async-done | bytes 1179680 | tf_op jit(solution)/shard_map/all_to_all | solution.py:92
  190.2 5.8 %all-to-all-start.3 = ((bf16[16,32,1152]{2,1,0:T(8,128)(2,1)}), bf16[16,32,1152]{2,1,0:T(8,128)(2,1)S(1)}, u32[]{:S(2)}, u32[]{:S(2)}) async-start(bf16[16,32,1152]{2,1,0:T(8,128)(2,1)} %concatenate.40), calls=%async_computation.3 | async-start | bytes 2359296 | tf_op jit(solution)/shard_map/all_to_all | solution.py:92
  196.2 28.2 %all-to-all-done.3 = bf16[16,32,1152]{2,1,0:T(8,128)(2,1)S(1)} async-done(((bf16[16,32,1152]{2,1,0:T(8,128)(2,1)}), bf16[16,32,1152]{2,1,0:T(8,128)(2,1)S(1)}, u32[]{:S(2)}, u32[]{:S(2)}) %all-to-all-start.3) | async-done | bytes 1179680 | tf_op jit(solution)/shard_map/all_to_all | solution.py:92
  227.1 2.2 reduce-scatter.2.cloned.1.call-done
  (74 shorter events, 13.5 us)
Async XLA Ops:
  7.2 4.5 %copy-start.3 = (bf16[256,1024]{1,0:T(8,128)(2,1)S(1)}, bf16[256,1024]{1,0:T(8,128)(2,1)}, u32[]{:S(2)}) copy-start(bf16[256,1024]{1,0:T(8,128)(2,1)} %param.6) | copy-start | bytes 1572868
  14.2 10.3 %copy-start.8 = (bf16[256,1024]{1,0:T(8,128)(2,1)S(1)}, bf16[256,1024]{1,0:T(8,128)(2,1)}, u32[]{:S(2)}) copy-start(bf16[256,1024]{1,0:T(8,128)(2,1)} %param.5) | copy-start | bytes 1572868
  14.2 56.1 %all-to-all-start.2 = ((bf16[16,32,2048]{2,1,0:T(8,128)(2,1)}), bf16[16,32,2048]{2,1,0:T(8,128)(2,1)S(1)}, u32[]{:S(2)}, u32[]{:S(2)}) async-start(bf16[16,32,2048]{2,1,0:T(8,128)(2,1)} %bitcast.125), calls=%async_computation.2 | async-start | bytes 4194304 | tf_op jit(solution)/shard_map/all_to_all | solution.py:89
  70.4 1.4 copy-start
  71.7 53.9 %all-to-all-start = ((bf16[16,32,2048]{2,1,0:T(8,128)(2,1)}), bf16[16,32,2048]{2,1,0:T(8,128)(2,1)S(1)}, u32[]{:S(2)}, u32[]{:S(2)}) async-start(bf16[16,32,2048]{2,1,0:T(8,128)(2,1)} %bitcast.126), calls=%async_computation | async-start | bytes 4194304 | tf_op jit(solution)/shard_map/all_to_all | solution.py:89
  78.1 151.2 %reduce-scatter.2.cloned.1.call-start = ((), (), s32[]{:S(2)}) async-start(), calls=%async_computation.5 | async-start | bytes 5013504 | tf_op jit(solution)/shard_map/reduce_scatter | solution.py:106
  78.3 4.1 %copy-start.1 = (bf16[16,32,2048]{2,1,0:T(8,128)(2,1)S(1)}, bf16[16,32,2048]{2,1,0:T(8,128)(2,1)}, u32[]{:S(2)}) copy-start(bf16[16,32,2048]{2,1,0:T(8,128)(2,1)} %copy-done) | copy-start | bytes 6291460
  133.4 1.1 copy-start.4
  133.5 1.2 copy-start.6
  135.7 1.6 copy-start.2
  135.7 2.0 copy-start.9
  135.7 2.5 %copy-start.10 = (f32[512,768]{1,0:T(8,128)S(1)}, f32[512,768]{1,0:T(8,128)}, u32[]{:S(2)}) copy-start(f32[512,768]{1,0:T(8,128)} %fusion.9) | copy-start | bytes 4718596
  147.2 1.1 copy-start.7
  148.3 2.5 %copy-start.5 = (bf16[512,768]{1,0:T(8,128)(2,1)S(1)}, bf16[512,768]{1,0:T(8,128)(2,1)}, u32[]{:S(2)}) copy-start(bf16[512,768]{1,0:T(8,128)(2,1)} %copy-done.4) | copy-start | bytes 2359300
  155.3 34.9 %all-to-all-start.1 = ((bf16[16,32,1152]{2,1,0:T(8,128)(2,1)}), bf16[16,32,1152]{2,1,0:T(8,128)(2,1)S(1)}, u32[]{:S(2)}, u32[]{:S(2)}) async-start(bf16[16,32,1152]{2,1,0:T(8,128)(2,1)} %concatenate.37), calls=%async_computation.1 | async-start | bytes 2359296 | tf_op jit(solution)/shard_map/all_to_all | solution.py:92
  190.2 34.3 %all-to-all-start.3 = ((bf16[16,32,1152]{2,1,0:T(8,128)(2,1)}), bf16[16,32,1152]{2,1,0:T(8,128)(2,1)S(1)}, u32[]{:S(2)}, u32[]{:S(2)}) async-start(bf16[16,32,1152]{2,1,0:T(8,128)(2,1)} %concatenate.40), calls=%async_computation.3 | async-start | bytes 2359296 | tf_op jit(solution)/shard_map/all_to_all | solution.py:92
Sparse Core Ops, SparseCore 0:
  147.3 81.8 reduce-scatter.1
where the time goes:
time: 239 us; the launch traced here: 236 us
  waiting for transfers between devices  134 us (56%)
  matrix products  39.1 us (16%)
  starting transfers between devices  27.4 us (11%)
  between operations  14.3 us (6%)
  local copies, waits for them, and re-layouts  11.3 us (5%)
  other arithmetic  9.97 us (4%)
    all_to_all x2, waiting for transfers between devices, on_device(): lax.all_to_all(payload, 'expert', 0, 0, tiled=True).reshape(-1, 2 * width)  82.6 us
    all_to_all x2, waiting for transfers between devices, on_device(): lax.all_to_all(back.reshape(n_expert, -1, width + PAD), 'expert', 0, 0, t...  49.2 us
    dot_general x12, matrix products, mm(): return jnp.dot(a, b, preferred_element_type=F32)  22.3 us
    all_to_all x2, starting transfers between devices, on_device(): lax.all_to_all(payload, 'expert', 0, 0, tiled=True).reshape(-1, 2 * width)  15 us
    all_to_all x2, starting transfers between devices, on_device(): lax.all_to_all(back.reshape(n_expert, -1, width + PAD), 'expert', 0, 0, t...  12.2 us
    dot_general x2, matrix products, expert_step(): lax.dot_general(grad_pre_gate, w_gate, CONTRACT_LAST, preferred_element_t...  4.9 us
    dot_general x2, matrix products, expert_step(): lax.dot_general(grad_pre_up, w_up, CONTRACT_LAST, preferred_element_type=...  4.9 us
  transfers between devices with their start and end apart: 5, of which 5 were waited for; matrix products, arithmetic and copies ran while one was open for 13% of the time, Pallas kernels for 0%

commit v1 on v0

--- a/solution.py
+++ b/solution.py
@@ -1,6 +1,8 @@
 import jax
 import jax.numpy as jnp
 from jax import lax
+from jax.experimental import pallas as pl
+from jax.experimental.pallas import tpu as pltpu
 from jax.sharding import PartitionSpec as P
 
 MICRO = 2
@@ -11,6 +13,7 @@
 
 CONTRACT_LAST = (((1,), (1,)), ((), ()))
 CONTRACT_FIRST = (((0,), (0,)), ((), ()))
+MESH = pl.DeviceIdType.MESH
 
 
 def mm(a, b):
@@ -60,16 +63,129 @@
     return jnp.concatenate([input_grad, tail], axis=1), grads
 
 
+def exchange_kernel(p0_ref, p1_ref, w_ref, ret0_ref, ret1_ref, grad_ref,
+                    r0, r1, b0, b1, send_sem, recv_sem):
+    n = lax.axis_size("expert")
+    me = lax.axis_index("expert")
+    row = lax.axis_index("dp")
+    chunk = p0_ref.shape[0] // n
+    width = w_ref.shape[1]
+
+    barrier = pltpu.get_barrier_semaphore()
+    for k in range(1, n):
+        peer = lax.rem(me + k, n)
+        pl.semaphore_signal(barrier, inc=1, device_id=(row, peer), device_id_type=MESH)
+    pl.semaphore_wait(barrier, n - 1)
+
+    def send(src, dst, phase):
+        mine = pl.ds(pl.multiple_of(me * chunk, chunk), chunk)
+        local = pltpu.make_async_copy(src.at[mine], dst.at[mine], recv_sem.at[phase])
+        local.start()
+        for k in range(1, n):
+            peer = lax.rem(me + k, n)
+            rows = pl.ds(pl.multiple_of(peer * chunk, chunk), chunk)
+            pltpu.make_async_remote_copy(
+                src_ref=src.at[rows],
+                dst_ref=dst.at[mine],
+                send_sem=send_sem.at[phase],
+                recv_sem=recv_sem.at[phase],
+                device_id=(row, peer),
+                device_id_type=MESH,
+            ).start()
+
+    def wait_recv(dst, phase):
+        pltpu.make_async_copy(dst, dst, recv_sem.at[phase]).wait()
+
+    def wait_send(src, phase):
+        rest = pl.ds(0, (n - 1) * chunk)
+        pltpu.make_async_copy(src.at[rest], src.at[rest], send_sem.at[phase]).wait()
+
+    def compute(recv, back, first):
+        rows_in = recv[:, :width]
+        scaled = recv[:, width:]
+        w_gate = w_ref[0]
+        w_up = w_ref[1]
+        w_down = w_ref[2]
+        pre_gate = mm(rows_in, w_gate)
+        pre_up = mm(rows_in, w_up)
+        sigmoid_gate = jax.nn.sigmoid(pre_gate)
+        activated = pre_gate * sigmoid_gate
+        hidden = (activated * pre_up).astype(BF16)
+        hidden_grad = mm(scaled, w_down)
+        gate_sum = jnp.sum(hidden.astype(F32) * hidden_grad, axis=1, keepdims=True)
+        grad_pre_gate = (
+            hidden_grad * pre_up * sigmoid_gate * (1.0 + pre_gate * (1.0 - sigmoid_gate))
+        ).astype(BF16)
+        grad_pre_up = (hidden_grad * activated).astype(BF16)
+        input_grad = (
+            lax.dot_general(grad_pre_gate, w_gate, CONTRACT_LAST, preferred_element_type=F32)
+            + lax.dot_general(grad_pre_up, w_up, CONTRACT_LAST, preferred_element_type=F32)
+        ).astype(BF16)
+        back[:, :width] = input_grad
+        high = gate_sum.astype(BF16).astype(F32)
+        low = gate_sum - high
+        column = lax.broadcasted_iota(jnp.int32, (recv.shape[0], PAD), 1)
+        tail = jnp.where(column == 0, high, jnp.where(column == 1, low, 0.0))
+        back[:, width:] = tail.astype(BF16)
+        grads = (
+            lax.dot_general(rows_in, grad_pre_gate, CONTRACT_FIRST, preferred_element_type=F32),
+            lax.dot_general(rows_in, grad_pre_up, CONTRACT_FIRST, preferred_element_type=F32),
+            lax.dot_general(scaled, hidden, CONTRACT_FIRST, preferred_element_type=F32),
+        )
+        for index, value in enumerate(grads):
+            if first:
+                grad_ref[index] = value
+            else:
+                grad_ref[index] += value
+
+    send(p0_ref, r0, 0)
+    wait_recv(r0, 0)
+    send(p1_ref, r1, 1)
+    compute(r0, b0, True)
+    send(b0, ret0_ref, 2)
+    wait_recv(r1, 1)
+    compute(r1, b1, False)
+    send(b1, ret1_ref, 3)
+    wait_recv(ret0_ref, 2)
+    wait_recv(ret1_ref, 3)
+    wait_send(p0_ref, 0)
+    wait_send(p1_ref, 1)
+    wait_send(b0, 2)
+    wait_send(b1, 3)
+
+
+def exchange(p0, p1, weights):
+    slots, full = p0.shape
+    width = weights.shape[1]
+    back = jax.ShapeDtypeStruct((slots, width + PAD), BF16)
+    vmem = pl.BlockSpec(memory_space=pltpu.VMEM)
+    return pl.pallas_call(
+        exchange_kernel,
+        out_shape=(back, back, jax.ShapeDtypeStruct(weights.shape, F32)),
+        in_specs=[vmem] * 3,
+        out_specs=(vmem, vmem, vmem),
+        scratch_shapes=[
+            pltpu.VMEM((slots, full), BF16),
+            pltpu.VMEM((slots, full), BF16),
+            pltpu.VMEM((slots, width + PAD), BF16),
+            pltpu.VMEM((slots, width + PAD), BF16),
+            pltpu.SemaphoreType.DMA((4,)),
+            pltpu.SemaphoreType.DMA((4,)),
+        ],
+        compiler_params=pltpu.CompilerParams(
+            collective_id=0, has_side_effects=True, vmem_limit_bytes=60 * 1024 * 1024
+        ),
+    )(p0, p1, weights)
+
+
 def on_device(tokens, cotangent, gates, expert_ids, expert_weights):
     n_expert = lax.axis_size("expert")
     expert_count = n_expert * expert_weights.shape[0]
     batch_rows = tokens.shape[0] // MICRO
     capacity = max(2, 4 * batch_rows // expert_count)
     width = tokens.shape[1]
-    w_gate, w_up, w_down = expert_weights[0, 0], expert_weights[0, 1], expert_weights[0, 2]
-
-    token_parts, gate_parts = [], []
-    totals = None
+
+    masks, gate_list, payloads = [], [], []
     for micro_index in range(MICRO):
         lower = micro_index * batch_rows
         upper = lower + batch_rows
@@ -83,15 +199,14 @@
         rows_scaled = (
             mm(first.astype(BF16), scaled_first) + mm(second.astype(BF16), scaled_second)
         ).astype(BF16)
-        payload = jnp.concatenate([rows_in, rows_scaled], axis=1).reshape(
-            n_expert, -1, 2 * width
-        )
-        recv = lax.all_to_all(payload, "expert", 0, 0, tiled=True).reshape(-1, 2 * width)
-        back, grads = expert_step(recv, w_gate, w_up, w_down, width)
-        totals = grads if totals is None else tuple(t + g for t, g in zip(totals, grads))
-        ret = lax.all_to_all(
-            back.reshape(n_expert, -1, width + PAD), "expert", 0, 0, tiled=True
-        ).reshape(-1, width + PAD)
+        payloads.append(jnp.concatenate([rows_in, rows_scaled], axis=1))
+        masks.append((first, second, both))
+        gate_list.append(gate)
+
+    ret0, ret1, totals = exchange(payloads[0], payloads[1], expert_weights[0])
+
+    token_parts, gate_parts = [], []
+    for (first, second, both), gate, ret in zip(masks, gate_list, (ret0, ret1)):
         token_grad = lax.dot_general(
             both, ret[:, :width], CONTRACT_FIRST, preferred_element_type=F32
         ).astype(BF16)
@@ -102,7 +217,7 @@
         token_parts.append(token_grad)
         gate_parts.append(gate_grad.astype(BF16))
 
-    rounded = jnp.stack(totals).astype(BF16)[None]
+    rounded = totals.astype(BF16)[None]
     weights_grad = lax.psum_scatter(rounded, "dp", scatter_dimension=2, tiled=True)
     return (
         jnp.concatenate(token_parts, axis=0),

time: 239 us -> 273 us (1.14)
  Pallas kernels: 0 us -> 159 us
  waiting for transfers between devices: 134 us -> 75.8 us
  matrix products: 39.1 us -> 4.54 us
  starting transfers between devices: 27.4 us -> 0.04 us
  local copies, waits for them, and re-layouts: 11.3 us -> 3.95 us
  other arithmetic: 9.97 us -> 13.8 us
    pallas_call x0 -> x1, Pallas kernels: none -> 159 us  [exchange(): pl.pallas_call(exchange_kernel, out_shape=(back, back, jax.ShapeDtypeStru...]
    all_to_all x4 -> x0, waiting for transfers between devices: 132 us -> none  [the longest x2 82.6 us: on_device(): lax.all_to_all(payload, 'expert', 0, 0, tiled=True).reshape(-1, 2 * width)]
    reduce_scatter x1, waiting for transfers between devices: 2.17 us -> 75.7 us  [on_device(): lax.psum_scatter(rounded, 'dp', scatter_dimension=2, tiled=True)]
    all_to_all x4 -> x0, starting transfers between devices: 27.2 us -> none  [the longest x2 15 us: on_device(): lax.all_to_all(payload, 'expert', 0, 0, tiled=True).reshape(-1, 2 * width)]
    dot_general x12 -> x6, matrix products: 22.3 us -> 3.85 us  [mm(): return jnp.dot(a, b, preferred_element_type=F32)]
    dot_general x10 -> x0, matrix products: 16.2 us -> none  [the longest x2 4.9 us: expert_step(): lax.dot_general(grad_pre_gate, w_gate, CONTRACT_LAST, preferred_element_t...]
    broadcast_in_dim x0 -> x1, other arithmetic: none -> 6.37 us  [on_device(): rounded = totals.astype(BF16)[None]]
    concatenate x3 -> x0, local copies, waits for them, and re-layouts: 4.12 us -> none  [expert_step(): return (jnp.concatenate([input_grad, tail], axis=1), grads)]
  transfers between devices with their start and end apart: 5 -> 1, of which waited for: 5 -> 1; matrix products, arithmetic and copies ran while one was open for 13% -> 1% of each run, Pallas kernels for 0% -> 0%
where the time goes in v1:
time: 273 us; the launch traced here: 271 us
  Pallas kernels  159 us (58%)
  waiting for transfers between devices  75.8 us (28%)
  between operations  14.2 us (5%)
  other arithmetic  13.8 us (5%)
  matrix products  4.54 us (2%)
  local copies, waits for them, and re-layouts  3.95 us (1%)
    pallas_call x1, Pallas kernels, exchange(): pl.pallas_call(exchange_kernel, out_shape=(back, back, jax.ShapeDtypeStru...  159 us
    reduce_scatter x1, waiting for transfers between devices, on_device(): lax.psum_scatter(rounded, 'dp', scatter_dimension=2, tiled=True)  75.7 us
    broadcast_in_dim x1, other arithmetic, on_device(): rounded = totals.astype(BF16)[None]  6.37 us
  transfers between devices with their start and end apart: 1, of which 1 were waited for; matrix products, arithmetic and copies ran while one was open for 1% of the time, Pallas kernels for 0%

profile of v1, /device:TPU:65, one launch (start us, length us, event | category | flops | bytes accessed | tf_op | source)
XLA Modules:
  0.0 270.8 jit_solution(7627156738300687744)
XLA Ops:
  7.2 0.7 fusion.52
  8.2 0.1 eq.115
  8.5 0.1 eq.127
  8.8 0.7 slice_convert_fusion
  9.5 0.6 reduce-window.14
  10.0 0.2 slice_reduce_fusion.5
  10.4 0.1 reduce_sum.67
  10.5 0.2 slice_reduce_fusion.2
  10.7 0.6 reduce-window.16
  11.3 0.2 slice_reduce_fusion.4
  11.7 0.1 reduce_sum.69
  11.8 0.2 slice_reduce_fusion
  12.0 1.5 fusion.10
  13.5 0.4 convolution_convert_fusion.1
  13.9 0.5 fusion.7
  14.4 0.4 convolution_convert_fusion
  14.9 0.5 add_convert_fusion.1
  15.4 1.5 pad_maximum_fusion.p0_ref
  16.9 0.5 add_convert_fusion
  17.4 1.6 pad_maximum_fusion.1.p1_ref
  19.0 158.6 %shard_map.76 = (bf16[512,1152]{1,0:T(8,128)(2,1)}, bf16[512,1152]{1,0:T(8,128)(2,1)}, f32[3,1024,768]{2,1,0:T(8,128)}) custom-call(bf16[512,2048]{1,0:T(8,128)(2,1)} %pad_maximum_fusion.p0_ref, bf16[512,2048]{1,0:T(8,128)(2,1)} %pad_maximum_fusion.1.p1_ref, bf16[3,1024,768]{2,1,0:T(8,128)(2,1)} %bitcast.65), custom_call_target="tpu_custom_call" | custom-call | tf_op jit(solution)/shard_map/pallas_call | solution.py:162
  177.6 6.4 %convert_bitcast_fusion = bf16[1,3,1024,768]{3,2,1,0:T(8,128)(2,1)} fusion(f32[3,1024,768]{2,1,0:T(8,128)} %get-tuple-element.8), kind=kLoop, calls=%fused_computation | loop fusion | flops 2359296 | bytes 14155776 | tf_op jit(solution)/shard_map/broadcast_in_dim | solution.py:220
  184.0 1.2 copy-done.2
  185.2 0.2 add_reduce_fusion.1
  185.6 0.2 add_reduce_fusion
  185.8 0.2 select_reduce_fusion.3
  186.0 0.2 select_reduce_fusion.1
  186.1 0.6 maximum_maximum_fusion
  186.7 0.4 convolution_convert_fusion.2
  187.1 0.3 convolution_convert_fusion.3
  187.4 0.8 pad_maximum_fusion.2
  188.3 75.7 %reduce-scatter.2.cloned.1.call-done = bf16[1,3,64,768]{3,2,1,0:T(8,128)(2,1)} async-done(((bf16[1,3,1024,768]{3,2,1,0:T(8,128)(2,1)}), bf16[1,3,64,768]{3,2,1,0:T(8,128)(2,1)}) %reduce-scatter.2.cloned.1.call-update) | async-done | bytes 294928 | tf_op jit(solution)/shard_map/reduce_scatter | solution.py:221
  (26 shorter events, 1.0 us)
Async XLA Ops:
  7.2 6.3 %copy-start.1 = (bf16[256,1024]{1,0:T(8,128)(2,1)S(1)}, bf16[256,1024]{1,0:T(8,128)(2,1)}, u32[]{:S(2)}) copy-start(bf16[256,1024]{1,0:T(8,128)(2,1)} %param.5) | copy-start | bytes 1572868
  7.2 256.8 %reduce-scatter.2.cloned.1.call-start = ((), (), s32[]{:S(2)}) async-start(), calls=%async_computation.1 | async-start | bytes 5013504 | tf_op jit(solution)/shard_map/reduce_scatter | solution.py:221
  10.7 3.2 %copy-start = (bf16[256,1024]{1,0:T(8,128)(2,1)S(1)}, bf16[256,1024]{1,0:T(8,128)(2,1)}, u32[]{:S(2)}) copy-start(bf16[256,1024]{1,0:T(8,128)(2,1)} %param.6) | copy-start | bytes 1572868
  184.0 1.3 copy-start.2
  184.0 1.6 copy-start.3
Sparse Core Ops, SparseCore 0:
  184.1 79.8 reduce-scatter.1

commit v2 on v1

--- a/solution.py
+++ b/solution.py
@@ -63,19 +63,24 @@
     return jnp.concatenate([input_grad, tail], axis=1), grads
 
 
-def exchange_kernel(p0_ref, p1_ref, w_ref, ret0_ref, ret1_ref, grad_ref,
-                    r0, r1, b0, b1, send_sem, recv_sem):
+def exchange_kernel(p0_ref, p1_ref, w_ref, ret0_ref, ret1_ref, out_ref,
+                    r0, r1, b0, b1, grad_ref, rounded, gathered, send_sem, recv_sem):
     n = lax.axis_size("expert")
     me = lax.axis_index("expert")
+    n_row = lax.axis_size("dp")
     row = lax.axis_index("dp")
     chunk = p0_ref.shape[0] // n
     width = w_ref.shape[1]
+    part = out_ref.shape[1]
 
     barrier = pltpu.get_barrier_semaphore()
     for k in range(1, n):
         peer = lax.rem(me + k, n)
         pl.semaphore_signal(barrier, inc=1, device_id=(row, peer), device_id_type=MESH)
-    pl.semaphore_wait(barrier, n - 1)
+    for k in range(1, n_row):
+        peer = lax.rem(row + k, n_row)
+        pl.semaphore_signal(barrier, inc=1, device_id=(peer, me), device_id_type=MESH)
+    pl.semaphore_wait(barrier, n - 1 + n_row - 1)
 
     def send(src, dst, phase):
         mine = pl.ds(pl.multiple_of(me * chunk, chunk), chunk)
@@ -146,22 +151,46 @@
     wait_recv(r1, 1)
     compute(r1, b1, False)
     send(b1, ret1_ref, 3)
+
+    rounded[...] = grad_ref[...].astype(BF16)
+    mine = pl.ds(pl.multiple_of(row * part, part), part)
+    pltpu.make_async_copy(rounded.at[:, mine], gathered.at[row], recv_sem.at[4]).start()
+    for k in range(1, n_row):
+        peer = lax.rem(row + k, n_row)
+        pltpu.make_async_remote_copy(
+            src_ref=rounded.at[:, pl.ds(pl.multiple_of(peer * part, part), part)],
+            dst_ref=gathered.at[row],
+            send_sem=send_sem.at[4],
+            recv_sem=recv_sem.at[4],
+            device_id=(peer, me),
+            device_id_type=MESH,
+        ).start()
+    pltpu.make_async_copy(gathered, gathered, recv_sem.at[4]).wait()
+    total = gathered[0].astype(F32)
+    for k in range(1, n_row):
+        total = total + gathered[k].astype(F32)
+    out_ref[...] = total.astype(BF16)
+
     wait_recv(ret0_ref, 2)
     wait_recv(ret1_ref, 3)
     wait_send(p0_ref, 0)
     wait_send(p1_ref, 1)
     wait_send(b0, 2)
     wait_send(b1, 3)
-
-
-def exchange(p0, p1, weights):
+    rest = pl.ds(0, n_row - 1)
+    pltpu.make_async_copy(gathered.at[rest], gathered.at[rest], send_sem.at[4]).wait()
+
+
+def exchange(p0, p1, weights, n_row):
     slots, full = p0.shape
     width = weights.shape[1]
+    part = width // n_row
     back = jax.ShapeDtypeStruct((slots, width + PAD), BF16)
+    share = (weights.shape[0], part, weights.shape[2])
     vmem = pl.BlockSpec(memory_space=pltpu.VMEM)
     return pl.pallas_call(
         exchange_kernel,
-        out_shape=(back, back, jax.ShapeDtypeStruct(weights.shape, F32)),
+        out_shape=(back, back, jax.ShapeDtypeStruct(share, BF16)),
         in_specs=[vmem] * 3,
         out_specs=(vmem, vmem, vmem),
         scratch_shapes=[
@@ -169,8 +198,11 @@
             pltpu.VMEM((slots, full), BF16),
             pltpu.VMEM((slots, width + PAD), BF16),
             pltpu.VMEM((slots, width + PAD), BF16),
-            pltpu.SemaphoreType.DMA((4,)),
-            pltpu.SemaphoreType.DMA((4,)),
+            pltpu.VMEM(weights.shape, F32),
+            pltpu.VMEM(weights.shape, BF16),
+            pltpu.VMEM((n_row,) + share, BF16),
+            pltpu.SemaphoreType.DMA((5,)),
+            pltpu.SemaphoreType.DMA((5,)),
         ],
         compiler_params=pltpu.CompilerParams(
             collective_id=0, has_side_effects=True, vmem_limit_bytes=60 * 1024 * 1024
@@ -203,7 +235,9 @@
         masks.append((first, second, both))
         gate_list.append(gate)
 
-    ret0, ret1, totals = exchange(payloads[0], payloads[1], expert_weights[0])
+    ret0, ret1, weights_grad = exchange(
+        payloads[0], payloads[1], expert_weights[0], lax.axis_size("dp")
+    )
 
     token_parts, gate_parts = [], []
     for (first, second, both), gate, ret in zip(masks, gate_list, (ret0, ret1)):
@@ -217,12 +251,10 @@
         token_parts.append(token_grad)
         gate_parts.append(gate_grad.astype(BF16))
 
-    rounded = totals.astype(BF16)[None]
-    weights_grad = lax.psum_scatter(rounded, "dp", scatter_dimension=2, tiled=True)
     return (
         jnp.concatenate(token_parts, axis=0),
         jnp.concatenate(gate_parts, axis=0),
-        weights_grad,
+        weights_grad[None],
     )
 
 

time: 273 us -> 207 us (0.76)
  waiting for transfers between devices: 75.8 us -> 0 us
  Pallas kernels: 159 us -> 188 us
  between operations: 14.2 us -> 0.83 us
  other arithmetic: 13.8 us -> 9.45 us
    reduce_scatter x1 -> x0, waiting for transfers between devices: 75.7 us -> none  [on_device(): lax.psum_scatter(rounded, 'dp', scatter_dimension=2, tiled=True)]
    pallas_call x1, Pallas kernels: 159 us -> 188 us  [exchange(): pl.pallas_call(exchange_kernel, out_shape=(back, back, jax.ShapeDtypeStru...]
    broadcast_in_dim x1 -> x0, other arithmetic: 6.37 us -> none  [on_device(): rounded = totals.astype(BF16)[None]]
  transfers between devices with their start and end apart: 1 -> 0, of which waited for: 1 -> 0; matrix products, arithmetic and copies ran while one was open for 1% -> 0% of each run, Pallas kernels for 0% -> 0%
where the time goes in v2:
time: 207 us
  Pallas kernels  188 us (91%)
  other arithmetic  9.45 us (5%)
  matrix products  5.81 us (3%)
  local copies, waits for them, and re-layouts  3.25 us (2%)
    pallas_call x1, Pallas kernels, exchange(): pl.pallas_call(exchange_kernel, out_shape=(back, back, jax.ShapeDtypeStru...  188 us

profile of v2, /device:TPU:65, one launch (start us, length us, event | category | flops | bytes accessed | tf_op | source)
XLA Modules:
  0.0 207.0 jit_solution(8103320990690199476)
XLA Ops:
  0.7 0.8 slice_convert_fusion
  1.4 0.7 fusion.52
  2.2 0.1 eq.131
  2.4 0.1 eq.127
  2.5 0.6 reduce-window.16
  3.1 0.2 slice_reduce_fusion.4
  3.4 0.1 reduce_sum.69
  3.6 0.2 slice_reduce_fusion
  3.9 0.1 eq.115
  4.1 0.1 eq.111
  4.2 0.6 reduce-window.14
  4.8 0.2 slice_reduce_fusion.5
  5.1 0.1 reduce_sum.67
  5.3 0.2 slice_reduce_fusion.2
  5.5 1.4 convolution_convert_fusion.1
  6.9 0.4 convolution_convert_fusion
  7.3 0.5 fusion.10
  7.8 0.5 add_convert_fusion.1
  8.3 1.5 pad_maximum_fusion.p0_ref
  9.9 0.5 fusion.7
  10.4 0.5 add_convert_fusion
  10.9 1.5 pad_maximum_fusion.1.p1_ref
  12.4 187.7 %shard_map.76 = (bf16[512,1152]{1,0:T(8,128)(2,1)}, bf16[512,1152]{1,0:T(8,128)(2,1)}, bf16[3,64,768]{2,1,0:T(8,128)(2,1)}) custom-call(bf16[512,2048]{1,0:T(8,128)(2,1)} %pad_maximum_fusion.p0_ref, bf16[512,2048]{1,0:T(8,128)(2,1)} %pad_maximum_fusion.1.p1_ref, bf16[3,1024,768]{2,1,0:T(8,128)(2,1)} %bitcast.64), custom_call_target="tpu_custom_call" | custom-call | tf_op jit(solution)/shard_map/pallas_call | solution.py:191
  200.1 1.3 add_reduce_fusion.1
  201.4 1.6 convolution_convert_fusion.3
  203.0 0.1 select_reduce_fusion.3
  203.2 1.2 add_reduce_fusion
  204.4 0.3 convolution_convert_fusion.2
  204.8 0.1 select_reduce_fusion.1
  204.9 0.6 maximum_maximum_fusion
  205.5 0.8 pad_maximum_fusion.2
  206.3 0.7 copy.27
  (23 shorter events, 0.6 us)
Async XLA Ops:
  0.6 6.7 %copy-start = (bf16[256,1024]{1,0:T(8,128)(2,1)S(1)}, bf16[256,1024]{1,0:T(8,128)(2,1)}, u32[]{:S(2)}) copy-start(bf16[256,1024]{1,0:T(8,128)(2,1)} %param.6) | copy-start | bytes 1572868
  0.6 6.2 %copy-start.1 = (bf16[256,1024]{1,0:T(8,128)(2,1)S(1)}, bf16[256,1024]{1,0:T(8,128)(2,1)}, u32[]{:S(2)}) copy-start(bf16[256,1024]{1,0:T(8,128)(2,1)} %param.5) | copy-start | bytes 1572868
  200.1 4.3 %copy-start.3 = (bf16[512,1152]{1,0:T(8,128)(2,1)S(1)}, bf16[512,1152]{1,0:T(8,128)(2,1)}, u32[]{:S(2)}) copy-start(bf16[512,1152]{1,0:T(8,128)(2,1)} %get-tuple-element.7) | copy-start | bytes 3538948
  201.4 4.9 %copy-start.2 = (bf16[3,64,768]{2,1,0:T(8,128)(2,1)S(1)}, bf16[3,64,768]{2,1,0:T(8,128)(2,1)}, u32[]{:S(2)}) copy-start(bf16[3,64,768]{2,1,0:T(8,128)(2,1)} %get-tuple-element.8) | copy-start | bytes 884740

commit v3 on v2

--- a/solution.py
+++ b/solution.py
@@ -6,6 +6,7 @@
 from jax.sharding import PartitionSpec as P
 
 MICRO = 2
+SPLITS = 2
 PAD = 128
 
 F32 = jnp.float32
@@ -64,14 +65,19 @@
 
 
 def exchange_kernel(p0_ref, p1_ref, w_ref, ret0_ref, ret1_ref, out_ref,
-                    r0, r1, b0, b1, grad_ref, rounded, gathered, send_sem, recv_sem):
+                    recv, back, grad_ref, rounded, gathered, send_sem, recv_sem):
     n = lax.axis_size("expert")
     me = lax.axis_index("expert")
     n_row = lax.axis_size("dp")
     row = lax.axis_index("dp")
-    chunk = p0_ref.shape[0] // n
+    phases = recv.shape[0]
+    splits = phases // MICRO
+    capacity = p0_ref.shape[0] // n
+    piece = capacity // splits
     width = w_ref.shape[1]
     part = out_ref.shape[1]
+    payloads = (p0_ref, p1_ref)
+    returns = (ret0_ref, ret1_ref)
 
     barrier = pltpu.get_barrier_semaphore()
     for k in range(1, n):
@@ -82,32 +88,60 @@
         pl.semaphore_signal(barrier, inc=1, device_id=(peer, me), device_id_type=MESH)
     pl.semaphore_wait(barrier, n - 1 + n_row - 1)
 
-    def send(src, dst, phase):
-        mine = pl.ds(pl.multiple_of(me * chunk, chunk), chunk)
-        local = pltpu.make_async_copy(src.at[mine], dst.at[mine], recv_sem.at[phase])
-        local.start()
+    def slot_rows(expert, phase):
+        start = expert * capacity + (phase % splits) * piece
+        return pl.ds(pl.multiple_of(start, piece), piece)
+
+    def held_rows(source):
+        return pl.ds(pl.multiple_of(source * piece, piece), piece)
+
+    def scatter(phase, src_rows, dst_rows, src, dst, sem):
+        pltpu.make_async_copy(src.at[src_rows(me)], dst.at[dst_rows(me)], recv_sem.at[sem]).start()
         for k in range(1, n):
             peer = lax.rem(me + k, n)
-            rows = pl.ds(pl.multiple_of(peer * chunk, chunk), chunk)
             pltpu.make_async_remote_copy(
-                src_ref=src.at[rows],
-                dst_ref=dst.at[mine],
-                send_sem=send_sem.at[phase],
-                recv_sem=recv_sem.at[phase],
+                src_ref=src.at[src_rows(peer)],
+                dst_ref=dst.at[dst_rows(me)],
+                send_sem=send_sem.at[sem],
+                recv_sem=recv_sem.at[sem],
                 device_id=(row, peer),
                 device_id_type=MESH,
             ).start()
 
-    def wait_recv(dst, phase):
-        pltpu.make_async_copy(dst, dst, recv_sem.at[phase]).wait()
-
-    def wait_send(src, phase):
-        rest = pl.ds(0, (n - 1) * chunk)
-        pltpu.make_async_copy(src.at[rest], src.at[rest], send_sem.at[phase]).wait()
-
-    def compute(recv, back, first):
-        rows_in = recv[:, :width]
-        scaled = recv[:, width:]
+    def send_forward(phase):
+        scatter(phase, lambda e: slot_rows(e, phase), held_rows,
+                payloads[phase // splits], recv.at[phase], phase)
+
+    def send_back(phase):
+        scatter(phase, held_rows, lambda e: slot_rows(e, phase),
+                back.at[phase], returns[phase // splits], phases + phase)
+
+    def wait_all(buf, sem):
+        pltpu.make_async_copy(buf, buf, recv_sem.at[sem]).wait()
+
+    def wait_sent(buf, sem):
+        rest = pl.ds(0, (n - 1) * piece)
+        pltpu.make_async_copy(buf.at[rest], buf.at[rest], send_sem.at[sem]).wait()
+
+    def scatter_grads():
+        rounded[...] = grad_ref[...].astype(BF16)
+        mine = pl.ds(pl.multiple_of(row * part, part), part)
+        pltpu.make_async_copy(rounded.at[:, mine], gathered.at[row], recv_sem.at[2 * phases]).start()
+        for k in range(1, n_row):
+            peer = lax.rem(row + k, n_row)
+            pltpu.make_async_remote_copy(
+                src_ref=rounded.at[:, pl.ds(pl.multiple_of(peer * part, part), part)],
+                dst_ref=gathered.at[row],
+                send_sem=send_sem.at[2 * phases],
+                recv_sem=recv_sem.at[2 * phases],
+                device_id=(peer, me),
+                device_id_type=MESH,
+            ).start()
+
+    def compute(phase):
+        held = recv.at[phase]
+        rows_in = held[:, :width]
+        scaled = held[:, width:]
         w_gate = w_ref[0]
         w_up = w_ref[1]
         w_down = w_ref[2]
@@ -122,71 +156,60 @@
             hidden_grad * pre_up * sigmoid_gate * (1.0 + pre_gate * (1.0 - sigmoid_gate))
         ).astype(BF16)
         grad_pre_up = (hidden_grad * activated).astype(BF16)
-        input_grad = (
-            lax.dot_general(grad_pre_gate, w_gate, CONTRACT_LAST, preferred_element_type=F32)
-            + lax.dot_general(grad_pre_up, w_up, CONTRACT_LAST, preferred_element_type=F32)
-        ).astype(BF16)
-        back[:, :width] = input_grad
-        high = gate_sum.astype(BF16).astype(F32)
-        low = gate_sum - high
-        column = lax.broadcasted_iota(jnp.int32, (recv.shape[0], PAD), 1)
-        tail = jnp.where(column == 0, high, jnp.where(column == 1, low, 0.0))
-        back[:, width:] = tail.astype(BF16)
         grads = (
             lax.dot_general(rows_in, grad_pre_gate, CONTRACT_FIRST, preferred_element_type=F32),
             lax.dot_general(rows_in, grad_pre_up, CONTRACT_FIRST, preferred_element_type=F32),
             lax.dot_general(scaled, hidden, CONTRACT_FIRST, preferred_element_type=F32),
         )
         for index, value in enumerate(grads):
-            if first:
+            if phase == 0:
                 grad_ref[index] = value
             else:
                 grad_ref[index] += value
-
-    send(p0_ref, r0, 0)
-    wait_recv(r0, 0)
-    send(p1_ref, r1, 1)
-    compute(r0, b0, True)
-    send(b0, ret0_ref, 2)
-    wait_recv(r1, 1)
-    compute(r1, b1, False)
-    send(b1, ret1_ref, 3)
-
-    rounded[...] = grad_ref[...].astype(BF16)
-    mine = pl.ds(pl.multiple_of(row * part, part), part)
-    pltpu.make_async_copy(rounded.at[:, mine], gathered.at[row], recv_sem.at[4]).start()
-    for k in range(1, n_row):
-        peer = lax.rem(row + k, n_row)
-        pltpu.make_async_remote_copy(
-            src_ref=rounded.at[:, pl.ds(pl.multiple_of(peer * part, part), part)],
-            dst_ref=gathered.at[row],
-            send_sem=send_sem.at[4],
-            recv_sem=recv_sem.at[4],
-            device_id=(peer, me),
-            device_id_type=MESH,
-        ).start()
-    pltpu.make_async_copy(gathered, gathered, recv_sem.at[4]).wait()
+        if phase == phases - 1:
+            scatter_grads()
+        input_grad = (
+            lax.dot_general(grad_pre_gate, w_gate, CONTRACT_LAST, preferred_element_type=F32)
+            + lax.dot_general(grad_pre_up, w_up, CONTRACT_LAST, preferred_element_type=F32)
+        ).astype(BF16)
+        out = back.at[phase]
+        out[:, :width] = input_grad
+        high = gate_sum.astype(BF16).astype(F32)
+        low = gate_sum - high
+        column = lax.broadcasted_iota(jnp.int32, (input_grad.shape[0], PAD), 1)
+        tail = jnp.where(column == 0, high, jnp.where(column == 1, low, 0.0))
+        out[:, width:] = tail.astype(BF16)
+
+    send_forward(0)
+    for phase in range(phases):
+        wait_all(recv.at[phase], phase)
+        if phase + 1 < phases:
+            send_forward(phase + 1)
+        compute(phase)
+        send_back(phase)
+
+    wait_all(gathered, 2 * phases)
     total = gathered[0].astype(F32)
     for k in range(1, n_row):
         total = total + gathered[k].astype(F32)
     out_ref[...] = total.astype(BF16)
 
-    wait_recv(ret0_ref, 2)
-    wait_recv(ret1_ref, 3)
-    wait_send(p0_ref, 0)
-    wait_send(p1_ref, 1)
-    wait_send(b0, 2)
-    wait_send(b1, 3)
+    for phase in range(phases):
+        wait_all(back.at[phase], phases + phase)
+        wait_sent(recv.at[phase], phase)
+        wait_sent(back.at[phase], phases + phase)
     rest = pl.ds(0, n_row - 1)
-    pltpu.make_async_copy(gathered.at[rest], gathered.at[rest], send_sem.at[4]).wait()
+    pltpu.make_async_copy(gathered.at[rest], gathered.at[rest], send_sem.at[2 * phases]).wait()
 
 
 def exchange(p0, p1, weights, n_row):
     slots, full = p0.shape
     width = weights.shape[1]
     part = width // n_row
+    held = slots // SPLITS
     back = jax.ShapeDtypeStruct((slots, width + PAD), BF16)
     share = (weights.shape[0], part, weights.shape[2])
+    phases = MICRO * SPLITS
     vmem = pl.BlockSpec(memory_space=pltpu.VMEM)
     return pl.pallas_call(
         exchange_kernel,
@@ -194,18 +217,16 @@
         in_specs=[vmem] * 3,
         out_specs=(vmem, vmem, vmem),
         scratch_shapes=[
-            pltpu.VMEM((slots, full), BF16),
-            pltpu.VMEM((slots, full), BF16),
-            pltpu.VMEM((slots, width + PAD), BF16),
-            pltpu.VMEM((slots, width + PAD), BF16),
+            pltpu.VMEM((phases, held, full), BF16),
+            pltpu.VMEM((phases, held, width + PAD), BF16),
             pltpu.VMEM(weights.shape, F32),
             pltpu.VMEM(weights.shape, BF16),
             pltpu.VMEM((n_row,) + share, BF16),
-            pltpu.SemaphoreType.DMA((5,)),
-            pltpu.SemaphoreType.DMA((5,)),
+            pltpu.SemaphoreType.DMA((2 * phases + 1,)),
+            pltpu.SemaphoreType.DMA((2 * phases + 1,)),
         ],
         compiler_params=pltpu.CompilerParams(
-            collective_id=0, has_side_effects=True, vmem_limit_bytes=60 * 1024 * 1024
+            collective_id=0, has_side_effects=True, vmem_limit_bytes=62 * 1024 * 1024
         ),
     )(p0, p1, weights)
 

time: 207 us -> 238 us (1.15); the launches traced: 207 us -> 236 us
  Pallas kernels: 188 us -> 216 us
    pallas_call x1, Pallas kernels: 188 us -> 216 us  [exchange(): pl.pallas_call(exchange_kernel, out_shape=(back, back, jax.ShapeDtypeStru...]
where the time goes in v3:
time: 238 us; the launch traced here: 236 us
  Pallas kernels  216 us (91%)
  other arithmetic  9.45 us (4%)
  matrix products  5.82 us (2%)
  local copies, waits for them, and re-layouts  3.25 us (1%)
    pallas_call x1, Pallas kernels, exchange(): pl.pallas_call(exchange_kernel, out_shape=(back, back, jax.ShapeDtypeStru...  216 us

profile of v3, /device:TPU:65, one launch (start us, length us, event | category | flops | bytes accessed | tf_op | source)
XLA Modules:
  0.0 235.6 jit_solution(11488065861864285416)
XLA Ops:
  0.7 0.8 slice_convert_fusion
  1.4 0.7 fusion.52
  2.2 0.1 eq.131
  2.4 0.1 eq.127
  2.5 0.6 reduce-window.16
  3.1 0.2 slice_reduce_fusion.4
  3.4 0.1 reduce_sum.69
  3.6 0.2 slice_reduce_fusion
  3.9 0.1 eq.115
  4.1 0.1 eq.111
  4.2 0.6 reduce-window.14
  4.8 0.2 slice_reduce_fusion.5
  5.1 0.1 reduce_sum.67
  5.3 0.2 slice_reduce_fusion.2
  5.5 1.4 convolution_convert_fusion.1
  6.9 0.4 convolution_convert_fusion
  7.3 0.5 fusion.10
  7.8 0.5 add_convert_fusion.1
  8.3 1.5 pad_maximum_fusion.p0_ref
  9.9 0.5 fusion.7
  10.4 0.5 add_convert_fusion
  10.9 1.5 pad_maximum_fusion.1.p1_ref
  12.4 216.3 %shard_map.76 = (bf16[512,1152]{1,0:T(8,128)(2,1)}, bf16[512,1152]{1,0:T(8,128)(2,1)}, bf16[3,64,768]{2,1,0:T(8,128)(2,1)}) custom-call(bf16[512,2048]{1,0:T(8,128)(2,1)} %pad_maximum_fusion.p0_ref, bf16[512,2048]{1,0:T(8,128)(2,1)} %pad_maximum_fusion.1.p1_ref, bf16[3,1024,768]{2,1,0:T(8,128)(2,1)} %bitcast.64), custom_call_target="tpu_custom_call" | custom-call | tf_op jit(solution)/shard_map/pallas_call | solution.py:214
  228.7 1.3 add_reduce_fusion.1
  230.0 1.6 convolution_convert_fusion.3
  231.6 0.1 select_reduce_fusion.3
  231.8 1.2 add_reduce_fusion
  233.0 0.4 convolution_convert_fusion.2
  233.4 0.1 select_reduce_fusion.1
  233.5 0.6 maximum_maximum_fusion
  234.1 0.8 pad_maximum_fusion.2
  234.9 0.7 copy.27
  (23 shorter events, 0.6 us)
Async XLA Ops:
  0.6 6.7 %copy-start = (bf16[256,1024]{1,0:T(8,128)(2,1)S(1)}, bf16[256,1024]{1,0:T(8,128)(2,1)}, u32[]{:S(2)}) copy-start(bf16[256,1024]{1,0:T(8,128)(2,1)} %param.6) | copy-start | bytes 1572868
  0.6 6.2 %copy-start.1 = (bf16[256,1024]{1,0:T(8,128)(2,1)S(1)}, bf16[256,1024]{1,0:T(8,128)(2,1)}, u32[]{:S(2)}) copy-start(bf16[256,1024]{1,0:T(8,128)(2,1)} %param.5) | copy-start | bytes 1572868
  228.7 4.3 %copy-start.3 = (bf16[512,1152]{1,0:T(8,128)(2,1)S(1)}, bf16[512,1152]{1,0:T(8,128)(2,1)}, u32[]{:S(2)}) copy-start(bf16[512,1152]{1,0:T(8,128)(2,1)} %get-tuple-element.7) | copy-start | bytes 3538948
  230.0 4.9 %copy-start.2 = (bf16[3,64,768]{2,1,0:T(8,128)(2,1)S(1)}, bf16[3,64,768]{2,1,0:T(8,128)(2,1)}, u32[]{:S(2)}) copy-start(bf16[3,64,768]{2,1,0:T(8,128)(2,1)} %get-tuple-element.8) | copy-start | bytes 884740

commit v4 on v3

--- a/solution.py
+++ b/solution.py
@@ -6,7 +6,7 @@
 from jax.sharding import PartitionSpec as P
 
 MICRO = 2
-SPLITS = 2
+SPLITS = 1
 PAD = 128
 
 F32 = jnp.float32

time: 238 us -> 205 us (0.86); the launches traced: 236 us -> 205 us
  Pallas kernels: 216 us -> 186 us
    pallas_call x1, Pallas kernels: 216 us -> 186 us  [exchange(): pl.pallas_call(exchange_kernel, out_shape=(back, back, jax.ShapeDtypeStru...]
where the time goes in v4:
time: 205 us
  Pallas kernels  186 us (91%)
  other arithmetic  9.45 us (5%)
  matrix products  5.82 us (3%)
  local copies, waits for them, and re-layouts  3.25 us (2%)
    pallas_call x1, Pallas kernels, exchange(): pl.pallas_call(exchange_kernel, out_shape=(back, back, jax.ShapeDtypeStru...  186 us

profile of v4, /device:TPU:65, one launch (start us, length us, event | category | flops | bytes accessed | tf_op | source)
XLA Modules:
  0.0 205.1 jit_solution(11576975014608469824)
XLA Ops:
  0.7 0.8 slice_convert_fusion
  1.4 0.7 fusion.52
  2.2 0.1 eq.131
  2.4 0.1 eq.127
  2.5 0.6 reduce-window.16
  3.1 0.2 slice_reduce_fusion.4
  3.4 0.1 reduce_sum.69
  3.6 0.2 slice_reduce_fusion
  3.9 0.1 eq.115
  4.1 0.1 eq.111
  4.2 0.6 reduce-window.14
  4.8 0.2 slice_reduce_fusion.5
  5.1 0.1 reduce_sum.67
  5.3 0.2 slice_reduce_fusion.2
  5.5 1.4 convolution_convert_fusion.1
  6.9 0.4 convolution_convert_fusion
  7.3 0.5 fusion.10
  7.8 0.5 add_convert_fusion.1
  8.3 1.5 pad_maximum_fusion.p0_ref
  9.9 0.5 fusion.7
  10.4 0.5 add_convert_fusion
  10.9 1.5 pad_maximum_fusion.1.p1_ref
  12.4 185.7 %shard_map.76 = (bf16[512,1152]{1,0:T(8,128)(2,1)}, bf16[512,1152]{1,0:T(8,128)(2,1)}, bf16[3,64,768]{2,1,0:T(8,128)(2,1)}) custom-call(bf16[512,2048]{1,0:T(8,128)(2,1)} %pad_maximum_fusion.p0_ref, bf16[512,2048]{1,0:T(8,128)(2,1)} %pad_maximum_fusion.1.p1_ref, bf16[3,1024,768]{2,1,0:T(8,128)(2,1)} %bitcast.64), custom_call_target="tpu_custom_call" | custom-call | tf_op jit(solution)/shard_map/pallas_call | solution.py:214
  198.1 1.3 add_reduce_fusion.1
  199.4 1.6 convolution_convert_fusion.3
  201.1 0.1 select_reduce_fusion.3
  201.2 1.2 add_reduce_fusion
  202.4 0.4 convolution_convert_fusion.2
  202.8 0.1 select_reduce_fusion.1
  203.0 0.6 maximum_maximum_fusion
  203.5 0.8 pad_maximum_fusion.2
  204.4 0.7 copy.27
  (23 shorter events, 0.6 us)
Async XLA Ops:
  0.6 6.7 %copy-start = (bf16[256,1024]{1,0:T(8,128)(2,1)S(1)}, bf16[256,1024]{1,0:T(8,128)(2,1)}, u32[]{:S(2)}) copy-start(bf16[256,1024]{1,0:T(8,128)(2,1)} %param.6) | copy-start | bytes 1572868
  0.6 6.2 %copy-start.1 = (bf16[256,1024]{1,0:T(8,128)(2,1)S(1)}, bf16[256,1024]{1,0:T(8,128)(2,1)}, u32[]{:S(2)}) copy-start(bf16[256,1024]{1,0:T(8,128)(2,1)} %param.5) | copy-start | bytes 1572868
  198.1 4.3 %copy-start.3 = (bf16[512,1152]{1,0:T(8,128)(2,1)S(1)}, bf16[512,1152]{1,0:T(8,128)(2,1)}, u32[]{:S(2)}) copy-start(bf16[512,1152]{1,0:T(8,128)(2,1)} %get-tuple-element.7) | copy-start | bytes 3538948
  199.4 4.9 %copy-start.2 = (bf16[3,64,768]{2,1,0:T(8,128)(2,1)S(1)}, bf16[3,64,768]{2,1,0:T(8,128)(2,1)}, u32[]{:S(2)}) copy-start(bf16[3,64,768]{2,1,0:T(8,128)(2,1)} %get-tuple-element.8) | copy-start | bytes 884740

commit v5 on v4

--- a/solution.py
+++ b/solution.py
@@ -7,6 +7,7 @@
 
 MICRO = 2
 SPLITS = 1
+SIDE = 4
 PAD = 128
 
 F32 = jnp.float32
@@ -65,7 +66,8 @@
 
 
 def exchange_kernel(p0_ref, p1_ref, w_ref, ret0_ref, ret1_ref, out_ref,
-                    recv, back, grad_ref, rounded, gathered, send_sem, recv_sem):
+                    recv, back, grad_ref, round_a, round_b, first_a, first_b,
+                    part_a, part_b, second_a, second_b, send_sem, recv_sem, rs_send, rs_recv):
     n = lax.axis_size("expert")
     me = lax.axis_index("expert")
     n_row = lax.axis_size("dp")
@@ -123,20 +125,56 @@
         rest = pl.ds(0, (n - 1) * piece)
         pltpu.make_async_copy(buf.at[rest], buf.at[rest], send_sem.at[sem]).wait()
 
-    def scatter_grads():
-        rounded[...] = grad_ref[...].astype(BF16)
-        mine = pl.ds(pl.multiple_of(row * part, part), part)
-        pltpu.make_async_copy(rounded.at[:, mine], gathered.at[row], recv_sem.at[2 * phases]).start()
-        for k in range(1, n_row):
-            peer = lax.rem(row + k, n_row)
+    side = SIDE
+    col_a, col_b = row % side, row // side
+    half = out_ref.shape[2] // 2
+
+    def x_peer(k):
+        return col_b * side + lax.rem(col_a + k, side)
+
+    def y_peer(k):
+        return lax.rem(col_b + k, side) * side + col_a
+
+    def spread(src, dst, index, peer_of, sem):
+        pltpu.make_async_copy(src.at[index], dst.at[index], rs_recv.at[sem]).start()
+        for k in range(1, side):
             pltpu.make_async_remote_copy(
-                src_ref=rounded.at[:, pl.ds(pl.multiple_of(peer * part, part), part)],
-                dst_ref=gathered.at[row],
-                send_sem=send_sem.at[2 * phases],
-                recv_sem=recv_sem.at[2 * phases],
-                device_id=(peer, me),
+                src_ref=src.at[lax.rem(index + k, side)],
+                dst_ref=dst.at[index],
+                send_sem=rs_send.at[sem],
+                recv_sem=rs_recv.at[sem],
+                device_id=(peer_of(k), me),
                 device_id_type=MESH,
             ).start()
+
+    def scatter_grads():
+        for block in range(n_row):
+            rounded = grad_ref[:, block * part:(block + 1) * part, :].astype(BF16)
+            round_a[block % side, block // side] = rounded[:, :, :half]
+            round_b[block // side, block % side] = rounded[:, :, half:]
+        spread(round_a, first_a, col_a, x_peer, 0)
+        spread(round_b, first_b, col_b, y_peer, 1)
+
+    def reduce_grads():
+        pltpu.make_async_copy(first_a, first_a, rs_recv.at[0]).wait()
+        total = first_a[0].astype(F32)
+        for k in range(1, side):
+            total = total + first_a[k].astype(F32)
+        part_a[...] = total
+        spread(part_a, second_a, col_b, y_peer, 2)
+        pltpu.make_async_copy(first_b, first_b, rs_recv.at[1]).wait()
+        total = first_b[0].astype(F32)
+        for k in range(1, side):
+            total = total + first_b[k].astype(F32)
+        part_b[...] = total
+        spread(part_b, second_b, col_a, x_peer, 3)
+        for second, columns, sem in ((second_a, slice(0, half), 2),
+                                     (second_b, slice(half, 2 * half), 3)):
+            pltpu.make_async_copy(second, second, rs_recv.at[sem]).wait()
+            total = second[0]
+            for k in range(1, side):
+                total = total + second[k]
+            out_ref[:, :, columns] = total.astype(BF16)
 
     def compute(phase):
         held = recv.at[phase]
@@ -188,18 +226,15 @@
         compute(phase)
         send_back(phase)
 
-    wait_all(gathered, 2 * phases)
-    total = gathered[0].astype(F32)
-    for k in range(1, n_row):
-        total = total + gathered[k].astype(F32)
-    out_ref[...] = total.astype(BF16)
+    reduce_grads()
 
     for phase in range(phases):
         wait_all(back.at[phase], phases + phase)
         wait_sent(recv.at[phase], phase)
         wait_sent(back.at[phase], phases + phase)
-    rest = pl.ds(0, n_row - 1)
-    pltpu.make_async_copy(gathered.at[rest], gathered.at[rest], send_sem.at[2 * phases]).wait()
+    rest = pl.ds(0, side - 1)
+    for sem, buf in enumerate((first_a, first_b, second_a, second_b)):
+        pltpu.make_async_copy(buf.at[rest], buf.at[rest], rs_send.at[sem]).wait()
 
 
 def exchange(p0, p1, weights, n_row):
@@ -209,6 +244,7 @@
     held = slots // SPLITS
     back = jax.ShapeDtypeStruct((slots, width + PAD), BF16)
     share = (weights.shape[0], part, weights.shape[2])
+    quarter = (weights.shape[0], part, weights.shape[2] // 2)
     phases = MICRO * SPLITS
     vmem = pl.BlockSpec(memory_space=pltpu.VMEM)
     return pl.pallas_call(
@@ -220,10 +256,18 @@
             pltpu.VMEM((phases, held, full), BF16),
             pltpu.VMEM((phases, held, width + PAD), BF16),
             pltpu.VMEM(weights.shape, F32),
-            pltpu.VMEM(weights.shape, BF16),
-            pltpu.VMEM((n_row,) + share, BF16),
-            pltpu.SemaphoreType.DMA((2 * phases + 1,)),
-            pltpu.SemaphoreType.DMA((2 * phases + 1,)),
+            pltpu.VMEM((SIDE, SIDE) + quarter, BF16),
+            pltpu.VMEM((SIDE, SIDE) + quarter, BF16),
+            pltpu.VMEM((SIDE, SIDE) + quarter, BF16),
+            pltpu.VMEM((SIDE, SIDE) + quarter, BF16),
+            pltpu.VMEM((SIDE,) + quarter, F32),
+            pltpu.VMEM((SIDE,) + quarter, F32),
+            pltpu.VMEM((SIDE,) + quarter, F32),
+            pltpu.VMEM((SIDE,) + quarter, F32),
+            pltpu.SemaphoreType.DMA((2 * phases,)),
+            pltpu.SemaphoreType.DMA((2 * phases,)),
+            pltpu.SemaphoreType.DMA((4,)),
+            pltpu.SemaphoreType.DMA((4,)),
         ],
         compiler_params=pltpu.CompilerParams(
             collective_id=0, has_side_effects=True, vmem_limit_bytes=62 * 1024 * 1024

time: 205 us -> 178 us (0.87)
  Pallas kernels: 186 us -> 158 us
    pallas_call x1, Pallas kernels: 186 us -> 158 us  [exchange(): pl.pallas_call(exchange_kernel, out_shape=(back, back, jax.ShapeDtypeStru...]
where the time goes in v5:
time: 178 us
  Pallas kernels  158 us (89%)
  other arithmetic  9.45 us (5%)
  matrix products  5.82 us (3%)
  local copies, waits for them, and re-layouts  3.25 us (2%)
    pallas_call x1, Pallas kernels, exchange(): pl.pallas_call(exchange_kernel, out_shape=(back, back, jax.ShapeDtypeStru...  158 us
    dot_general x6, matrix products, mm(): return jnp.dot(a, b, preferred_element_type=F32)  3.85 us

profile of v5, /device:TPU:65, one launch (start us, length us, event | category | flops | bytes accessed | tf_op | source)
XLA Modules:
  0.0 177.6 jit_solution(9674813484169331172)
XLA Ops:
  0.7 0.8 slice_convert_fusion
  1.4 0.7 fusion.52
  2.2 0.1 eq.131
  2.4 0.1 eq.127
  2.5 0.6 reduce-window.16
  3.1 0.2 slice_reduce_fusion.4
  3.4 0.1 reduce_sum.69
  3.6 0.2 slice_reduce_fusion
  3.9 0.1 eq.115
  4.1 0.1 eq.111
  4.2 0.6 reduce-window.14
  4.8 0.2 slice_reduce_fusion.5
  5.1 0.1 reduce_sum.67
  5.3 0.2 slice_reduce_fusion.2
  5.5 1.4 convolution_convert_fusion.1
  6.9 0.4 convolution_convert_fusion
  7.3 0.5 fusion.10
  7.8 0.5 add_convert_fusion.1
  8.3 1.5 pad_maximum_fusion.p0_ref
  9.9 0.5 fusion.7
  10.4 0.5 add_convert_fusion
  10.9 1.5 pad_maximum_fusion.1.p1_ref
  12.4 158.2 %shard_map.76 = (bf16[512,1152]{1,0:T(8,128)(2,1)}, bf16[512,1152]{1,0:T(8,128)(2,1)}, bf16[3,64,768]{2,1,0:T(8,128)(2,1)}) custom-call(bf16[512,2048]{1,0:T(8,128)(2,1)} %pad_maximum_fusion.p0_ref, bf16[512,2048]{1,0:T(8,128)(2,1)} %pad_maximum_fusion.1.p1_ref, bf16[3,1024,768]{2,1,0:T(8,128)(2,1)} %bitcast.64), custom_call_target="tpu_custom_call" | custom-call | tf_op jit(solution)/shard_map/pallas_call | solution.py:250
  170.6 1.3 add_reduce_fusion.1
  171.9 1.6 convolution_convert_fusion.3
  173.6 0.1 select_reduce_fusion.3
  173.7 1.2 add_reduce_fusion
  174.9 0.4 convolution_convert_fusion.2
  175.3 0.1 select_reduce_fusion.1
  175.4 0.6 maximum_maximum_fusion
  176.0 0.8 pad_maximum_fusion.2
  176.8 0.7 copy.27
  (23 shorter events, 0.6 us)
Async XLA Ops:
  0.6 6.7 %copy-start = (bf16[256,1024]{1,0:T(8,128)(2,1)S(1)}, bf16[256,1024]{1,0:T(8,128)(2,1)}, u32[]{:S(2)}) copy-start(bf16[256,1024]{1,0:T(8,128)(2,1)} %param.6) | copy-start | bytes 1572868
  0.6 6.2 %copy-start.1 = (bf16[256,1024]{1,0:T(8,128)(2,1)S(1)}, bf16[256,1024]{1,0:T(8,128)(2,1)}, u32[]{:S(2)}) copy-start(bf16[256,1024]{1,0:T(8,128)(2,1)} %param.5) | copy-start | bytes 1572868
  170.6 4.3 %copy-start.3 = (bf16[512,1152]{1,0:T(8,128)(2,1)S(1)}, bf16[512,1152]{1,0:T(8,128)(2,1)}, u32[]{:S(2)}) copy-start(bf16[512,1152]{1,0:T(8,128)(2,1)} %get-tuple-element.7) | copy-start | bytes 3538948
  171.9 4.9 %copy-start.2 = (bf16[3,64,768]{2,1,0:T(8,128)(2,1)S(1)}, bf16[3,64,768]{2,1,0:T(8,128)(2,1)}, u32[]{:S(2)}) copy-start(bf16[3,64,768]{2,1,0:T(8,128)(2,1)} %get-tuple-element.8) | copy-start | bytes 884740

commit v6 on v5

--- a/solution.py
+++ b/solution.py
@@ -65,7 +65,7 @@
     return jnp.concatenate([input_grad, tail], axis=1), grads
 
 
-def exchange_kernel(p0_ref, p1_ref, w_ref, ret0_ref, ret1_ref, out_ref,
+def exchange_kernel(x0_ref, q0_ref, x1_ref, q1_ref, w_ref, ret0_ref, ret1_ref, out_ref,
                     recv, back, grad_ref, round_a, round_b, first_a, first_b,
                     part_a, part_b, second_a, second_b, send_sem, recv_sem, rs_send, rs_recv):
     n = lax.axis_size("expert")
@@ -74,11 +74,11 @@
     row = lax.axis_index("dp")
     phases = recv.shape[0]
     splits = phases // MICRO
-    capacity = p0_ref.shape[0] // n
+    capacity = x0_ref.shape[0] // n
     piece = capacity // splits
     width = w_ref.shape[1]
     part = out_ref.shape[1]
-    payloads = (p0_ref, p1_ref)
+    payloads = ((x0_ref, q0_ref), (x1_ref, q1_ref))
     returns = (ret0_ref, ret1_ref)
 
     barrier = pltpu.get_barrier_semaphore()
@@ -111,8 +111,10 @@
             ).start()
 
     def send_forward(phase):
-        scatter(phase, lambda e: slot_rows(e, phase), held_rows,
-                payloads[phase // splits], recv.at[phase], phase)
+        for index, src in enumerate(payloads[phase // splits]):
+            columns = pl.ds(index * width, width)
+            scatter(phase, lambda e: slot_rows(e, phase), held_rows,
+                    src, recv.at[phase, :, columns], phase)
 
     def send_back(phase):
         scatter(phase, held_rows, lambda e: slot_rows(e, phase),
@@ -237,8 +239,8 @@
         pltpu.make_async_copy(buf.at[rest], buf.at[rest], rs_send.at[sem]).wait()
 
 
-def exchange(p0, p1, weights, n_row):
-    slots, full = p0.shape
+def exchange(x0, q0, x1, q1, weights, n_row):
+    slots, full = x0.shape[0], 2 * x0.shape[1]
     width = weights.shape[1]
     part = width // n_row
     held = slots // SPLITS
@@ -250,7 +252,7 @@
     return pl.pallas_call(
         exchange_kernel,
         out_shape=(back, back, jax.ShapeDtypeStruct(share, BF16)),
-        in_specs=[vmem] * 3,
+        in_specs=[vmem] * 5,
         out_specs=(vmem, vmem, vmem),
         scratch_shapes=[
             pltpu.VMEM((phases, held, full), BF16),
@@ -272,7 +274,7 @@
         compiler_params=pltpu.CompilerParams(
             collective_id=0, has_side_effects=True, vmem_limit_bytes=62 * 1024 * 1024
         ),
-    )(p0, p1, weights)
+    )(x0, q0, x1, q1, weights)
 
 
 def on_device(tokens, cotangent, gates, expert_ids, expert_weights):
@@ -296,13 +298,11 @@
         rows_scaled = (
             mm(first.astype(BF16), scaled_first) + mm(second.astype(BF16), scaled_second)
         ).astype(BF16)
-        payloads.append(jnp.concatenate([rows_in, rows_scaled], axis=1))
+        payloads += [rows_in, rows_scaled]
         masks.append((first, second, both))
         gate_list.append(gate)
 
-    ret0, ret1, weights_grad = exchange(
-        payloads[0], payloads[1], expert_weights[0], lax.axis_size("dp")
-    )
+    ret0, ret1, weights_grad = exchange(*payloads, expert_weights[0], lax.axis_size("dp"))
 
     token_parts, gate_parts = [], []
     for (first, second, both), gate, ret in zip(masks, gate_list, (ret0, ret1)):

time: 178 us -> 181 us (1.017)
  matrix products: 5.82 us -> 9.77 us
  other arithmetic: 9.45 us -> 6.43 us
  Pallas kernels: 158 us -> 161 us
    dot_general x6, matrix products: 3.85 us -> 7.8 us  [mm(): return jnp.dot(a, b, preferred_element_type=F32)]
    concatenate x2 -> x0, other arithmetic: 3.02 us -> none  [on_device(): payloads.append(jnp.concatenate([rows_in, rows_scaled], axis=1))]
    pallas_call x1, Pallas kernels: 158 us -> 161 us  [exchange(): pl.pallas_call(exchange_kernel, out_shape=(back, back, jax.ShapeDtypeStru...]
where the time goes in v6:
time: 181 us
  Pallas kernels  161 us (89%)
  matrix products  9.77 us (5%)
  other arithmetic  6.43 us (4%)
  local copies, waits for them, and re-layouts  3.25 us (2%)
    pallas_call x1, Pallas kernels, exchange(): pl.pallas_call(exchange_kernel, out_shape=(back, back, jax.ShapeDtypeStru...  161 us
    dot_general x6, matrix products, mm(): return jnp.dot(a, b, preferred_element_type=F32)  7.8 us

profile of v6, /device:TPU:65, one launch (start us, length us, event | category | flops | bytes accessed | tf_op | source)
XLA Modules:
  0.0 181.2 jit_solution(11853594901367080079)
XLA Ops:
  0.7 0.8 slice_convert_fusion
  1.4 0.7 fusion.52
  2.1 0.1 copy.21
  2.2 0.1 eq.131
  2.4 0.1 eq.127
  2.5 0.6 reduce-window.16
  3.1 0.2 slice_reduce_fusion.4
  3.4 0.1 reduce_sum.69
  3.6 0.2 slice_reduce_fusion.1
  3.8 0.1 copy.20
  3.9 0.1 eq.115
  4.1 0.1 eq.111
  4.2 0.6 reduce-window.14
  4.8 0.2 slice_reduce_fusion.5
  5.1 0.1 reduce_sum.67
  5.3 0.2 slice_reduce_fusion.3
  5.5 2.4 %convolution_convert_fusion.1.x0_ref = bf16[512,1024]{1,0:T(8,128)(2,1)} fusion(bf16[256,1024]{1,0:T(8,128)(2,1)} %param.5, s32[128]{0:T(128)S(1)} %get-tuple-element.12, s32[128]{0:T(128)S(1)} %get-tuple-element.11), kind=kOutput, calls=%fused_computation.3 | convolution fusion | flops 134938624 | bytes 1311744 | tf_op jit(solution)/shard_map/dot_general | solution.py:22
  7.8 1.4 convolution_convert_fusion.x1_ref
  9.2 0.5 fusion.10
  9.7 1.5 add_convert_fusion.1.q0_ref
  11.3 0.5 fusion.7
  11.8 1.5 add_convert_fusion.q1_ref
  13.3 161.0 %shard_map.76 = (bf16[512,1152]{1,0:T(8,128)(2,1)}, bf16[512,1152]{1,0:T(8,128)(2,1)}, bf16[3,64,768]{2,1,0:T(8,128)(2,1)}) custom-call(bf16[512,1024]{1,0:T(8,128)(2,1)} %convolution_convert_fusion.1.x0_ref, bf16[512,1024]{1,0:T(8,128)(2,1)} %add_convert_fusion.1.q0_ref, bf16[512,1024]{1,0:T(8,128)(2,1)} %convolution_convert_fusion.x1_ref, ...), custom_call_target="tpu_custom_call" | custom-call | tf_op jit(solution)/shard_map/pallas_call | solution.py:252
  174.3 1.3 add_reduce_fusion.1
  175.6 1.6 convolution_convert_fusion.3
  177.2 0.1 select_reduce_fusion.3
  177.3 1.2 add_reduce_fusion
  178.6 0.3 convolution_convert_fusion.2
  178.9 0.1 select_reduce_fusion.1
  179.1 0.6 maximum_maximum_fusion
  179.6 0.8 pad_maximum_fusion
  180.5 0.7 copy.27
  (21 shorter events, 0.3 us)
Async XLA Ops:
  0.6 8.6 %copy-start = (bf16[256,1024]{1,0:T(8,128)(2,1)S(1)}, bf16[256,1024]{1,0:T(8,128)(2,1)}, u32[]{:S(2)}) copy-start(bf16[256,1024]{1,0:T(8,128)(2,1)} %param.6) | copy-start | bytes 1572868
  0.6 7.2 %copy-start.1 = (bf16[256,1024]{1,0:T(8,128)(2,1)S(1)}, bf16[256,1024]{1,0:T(8,128)(2,1)}, u32[]{:S(2)}) copy-start(bf16[256,1024]{1,0:T(8,128)(2,1)} %param.5) | copy-start | bytes 1572868
  174.2 4.3 %copy-start.3 = (bf16[512,1152]{1,0:T(8,128)(2,1)S(1)}, bf16[512,1152]{1,0:T(8,128)(2,1)}, u32[]{:S(2)}) copy-start(bf16[512,1152]{1,0:T(8,128)(2,1)} %get-tuple-element.7) | copy-start | bytes 3538948
  175.5 4.9 %copy-start.2 = (bf16[3,64,768]{2,1,0:T(8,128)(2,1)S(1)}, bf16[3,64,768]{2,1,0:T(8,128)(2,1)}, u32[]{:S(2)}) copy-start(bf16[3,64,768]{2,1,0:T(8,128)(2,1)} %get-tuple-element.8) | copy-start | bytes 884740

commit v7 on v5

--- a/solution.py
+++ b/solution.py
@@ -65,8 +65,10 @@
     return jnp.concatenate([input_grad, tail], axis=1), grads
 
 
-def exchange_kernel(p0_ref, p1_ref, w_ref, ret0_ref, ret1_ref, out_ref,
-                    recv, back, grad_ref, round_a, round_b, first_a, first_b,
+def exchange_kernel(p0_ref, both1_ref, first1_ref, second1_ref, x1_ref, qa1_ref, qb1_ref,
+                    both0_ref, first0_ref, second0_ref, w_ref,
+                    ret1_ref, out_ref, tg0_ref, gs0_ref,
+                    p1, ret0, recv, back, grad_ref, round_a, round_b, first_a, first_b,
                     part_a, part_b, second_a, second_b, send_sem, recv_sem, rs_send, rs_recv):
     n = lax.axis_size("expert")
     me = lax.axis_index("expert")
@@ -78,8 +80,8 @@
     piece = capacity // splits
     width = w_ref.shape[1]
     part = out_ref.shape[1]
-    payloads = (p0_ref, p1_ref)
-    returns = (ret0_ref, ret1_ref)
+    payloads = (p0_ref, p1)
+    returns = (ret0, ret1_ref)
 
     barrier = pltpu.get_barrier_semaphore()
     for k in range(1, n):
@@ -219,6 +221,10 @@
         out[:, width:] = tail.astype(BF16)
 
     send_forward(0)
+    p1[:, :width] = mm(both1_ref[...], x1_ref[...]).astype(BF16)
+    p1[:, width:] = (
+        mm(first1_ref[...], qa1_ref[...]) + mm(second1_ref[...], qb1_ref[...])
+    ).astype(BF16)
     for phase in range(phases):
         wait_all(recv.at[phase], phase)
         if phase + 1 < phases:
@@ -226,10 +232,22 @@
         compute(phase)
         send_back(phase)
 
+    wait_all(back.at[0], phases)
+    held = ret0[...]
+    tg0_ref[...] = lax.dot_general(
+        both0_ref[...], held[:, :width], CONTRACT_FIRST, preferred_element_type=F32
+    ).astype(BF16)
+    gate_sum = held[:, width:width + 1].astype(F32) + held[:, width + 1:width + 2].astype(F32)
+    for index, mask in enumerate((first0_ref, second0_ref)):
+        chosen = mask[...].astype(F32) > 0.5
+        gs0_ref[index:index + 1, :] = jnp.sum(
+            jnp.where(chosen, gate_sum, 0.0), axis=0, keepdims=True
+        )
     reduce_grads()
 
     for phase in range(phases):
-        wait_all(back.at[phase], phases + phase)
+        if phase > 0:
+            wait_all(back.at[phase], phases + phase)
         wait_sent(recv.at[phase], phase)
         wait_sent(back.at[phase], phases + phase)
     rest = pl.ds(0, side - 1)
@@ -237,8 +255,9 @@
         pltpu.make_async_copy(buf.at[rest], buf.at[rest], rs_send.at[sem]).wait()
 
 
-def exchange(p0, p1, weights, n_row):
+def exchange(p0, packing, unpacking, weights, n_row):
     slots, full = p0.shape
+    batch_rows = packing[3].shape[0]
     width = weights.shape[1]
     part = width // n_row
     held = slots // SPLITS
@@ -249,10 +268,17 @@
     vmem = pl.BlockSpec(memory_space=pltpu.VMEM)
     return pl.pallas_call(
         exchange_kernel,
-        out_shape=(back, back, jax.ShapeDtypeStruct(share, BF16)),
-        in_specs=[vmem] * 3,
-        out_specs=(vmem, vmem, vmem),
+        out_shape=(
+            back,
+            jax.ShapeDtypeStruct(share, BF16),
+            jax.ShapeDtypeStruct((batch_rows, width), BF16),
+            jax.ShapeDtypeStruct((2, batch_rows), F32),
+        ),
+        in_specs=[vmem] * 11,
+        out_specs=(vmem, vmem, vmem, vmem),
         scratch_shapes=[
+            pltpu.VMEM((slots, full), BF16),
+            pltpu.VMEM((slots, width + PAD), BF16),
             pltpu.VMEM((phases, held, full), BF16),
             pltpu.VMEM((phases, held, width + PAD), BF16),
             pltpu.VMEM(weights.shape, F32),
@@ -272,7 +298,7 @@
         compiler_params=pltpu.CompilerParams(
             collective_id=0, has_side_effects=True, vmem_limit_bytes=62 * 1024 * 1024
         ),
-    )(p0, p1, weights)
+    )(p0, *packing, *unpacking, weights)
 
 
 def on_device(tokens, cotangent, gates, expert_ids, expert_weights):
@@ -282,7 +308,7 @@
     capacity = max(2, 4 * batch_rows // expert_count)
     width = tokens.shape[1]
 
-    masks, gate_list, payloads = [], [], []
+    masks, gate_list, parts = [], [], []
     for micro_index in range(MICRO):
         lower = micro_index * batch_rows
         upper = lower + batch_rows
@@ -292,29 +318,39 @@
         gate = gates[lower:upper].astype(F32)
         scaled_first = (gate[:, 0:1] * cot).astype(BF16)
         scaled_second = (gate[:, 1:2] * cot).astype(BF16)
-        rows_in = mm(both, tokens[lower:upper]).astype(BF16)
-        rows_scaled = (
-            mm(first.astype(BF16), scaled_first) + mm(second.astype(BF16), scaled_second)
-        ).astype(BF16)
-        payloads.append(jnp.concatenate([rows_in, rows_scaled], axis=1))
         masks.append((first, second, both))
         gate_list.append(gate)
-
-    ret0, ret1, weights_grad = exchange(
-        payloads[0], payloads[1], expert_weights[0], lax.axis_size("dp")
-    )
-
-    token_parts, gate_parts = [], []
-    for (first, second, both), gate, ret in zip(masks, gate_list, (ret0, ret1)):
-        token_grad = lax.dot_general(
-            both, ret[:, :width], CONTRACT_FIRST, preferred_element_type=F32
-        ).astype(BF16)
-        gate_sum = ret[:, width].astype(F32) + ret[:, width + 1].astype(F32)
-        sum_first = jnp.sum(jnp.where(first, gate_sum[:, None], 0.0), axis=0)
-        sum_second = jnp.sum(jnp.where(second, gate_sum[:, None], 0.0), axis=0)
-        gate_grad = jnp.stack([sum_first / gate[:, 0], sum_second / gate[:, 1]], axis=1)
-        token_parts.append(token_grad)
-        gate_parts.append(gate_grad.astype(BF16))
+        parts.append((tokens[lower:upper], scaled_first, scaled_second))
+
+    first, second, both = masks[0]
+    rows_in, scaled_first, scaled_second = parts[0]
+    rows_in = mm(both, rows_in).astype(BF16)
+    rows_scaled = (
+        mm(first.astype(BF16), scaled_first) + mm(second.astype(BF16), scaled_second)
+    ).astype(BF16)
+    p0 = jnp.concatenate([rows_in, rows_scaled], axis=1)
+    first, second, both = masks[1]
+    packing = (both, first.astype(BF16), second.astype(BF16)) + parts[1]
+    first, second, both = masks[0]
+    unpacking = (both, first.astype(BF16), second.astype(BF16))
+
+    ret1, weights_grad, token_first, gate_sums = exchange(
+        p0, packing, unpacking, expert_weights[0], lax.axis_size("dp")
+    )
+
+    gate = gate_list[0]
+    gate_first = jnp.stack([gate_sums[0] / gate[:, 0], gate_sums[1] / gate[:, 1]], axis=1)
+    token_parts, gate_parts = [token_first], [gate_first.astype(BF16)]
+    (first, second, both), gate = masks[1], gate_list[1]
+    token_grad = lax.dot_general(
+        both, ret1[:, :width], CONTRACT_FIRST, preferred_element_type=F32
+    ).astype(BF16)
+    gate_sum = ret1[:, width].astype(F32) + ret1[:, width + 1].astype(F32)
+    sum_first = jnp.sum(jnp.where(first, gate_sum[:, None], 0.0), axis=0)
+    sum_second = jnp.sum(jnp.where(second, gate_sum[:, None], 0.0), axis=0)
+    gate_grad = jnp.stack([sum_first / gate[:, 0], sum_second / gate[:, 1]], axis=1)
+    token_parts.append(token_grad)
+    gate_parts.append(gate_grad.astype(BF16))
 
     return (
         jnp.concatenate(token_parts, axis=0),

time: 178 us -> 178 us (level)
  matrix products: 5.82 us -> 3.97 us
    convert_element_type x0 -> x3, other arithmetic: none -> 2.62 us  [the longest x1 0.95 us: on_device(): scaled_second = (gate[:, 1:2] * cot).astype(BF16)]
    dot_general x6 -> x3, matrix products: 3.85 us -> 2.39 us  [mm(): return jnp.dot(a, b, preferred_element_type=F32)]
where the time goes in v7:
time: 178 us
  Pallas kernels  158 us (89%)
  other arithmetic  10.8 us (6%)
  local copies, waits for them, and re-layouts  4.52 us (3%)
  matrix products  3.97 us (2%)
    pallas_call x1, Pallas kernels, exchange(): pl.pallas_call(exchange_kernel, out_shape=(back, jax.ShapeDtypeStruct(sha...  158 us

profile of v7, /device:TPU:65, one launch (start us, length us, event | category | flops | bytes accessed | tf_op | source)
XLA Modules:
  0.0 177.9 jit_solution(2602333062225209355)
XLA Ops:
  0.6 0.8 fusion.41
  1.4 0.1 copy.16
  1.5 0.1 eq.115
  1.7 0.6 reduce-window.14
  2.3 0.2 slice_reduce_fusion.5
  2.5 0.1 eq.111
  2.7 0.1 reduce_sum.45
  2.9 0.2 slice_reduce_fusion.2
  3.1 0.7 slice_convert_fusion
  3.8 1.5 fusion.6
  5.2 0.5 add_convert_fusion
  5.8 0.5 copy-done.1
  6.3 0.4 convolution_convert_fusion
  6.7 1.5 pad_maximum_fusion.p0_ref
  8.4 0.1 eq.131
  8.5 0.6 reduce-window.16
  9.1 0.2 slice_reduce_fusion.4
  9.3 0.1 eq.127
  9.6 0.1 reduce_sum.47
  9.7 0.2 slice_reduce_fusion.1
  9.9 0.8 fusion.8
  10.7 0.8 fusion.14
  11.6 0.9 fusion.4
  12.5 0.7 slice.94.x1_ref
  13.3 157.9 %shard_map.76 = (bf16[512,1152]{1,0:T(8,128)(2,1)}, bf16[3,64,768]{2,1,0:T(8,128)(2,1)}, bf16[128,1024]{1,0:T(8,128)(2,1)}, f32[2,128]{1,0:T(2,128)}) custom-call(bf16[512,2048]{1,0:T(8,128)(2,1)} %pad_maximum_fusion.p0_ref, bf16[512,128]{1,0:T(8,128)(2,1)} %get-tuple-element.35.both1_ref, bf16[512,128]{1,0:T(8,128)(2,1)} %get-tuple-element.36.first1_ref, ...), custom_call_target="tpu_custom_call" | custom-call | tf_op jit(solution)/shard_map/pallas_call | solution.py:269
  171.1 1.2 add_reduce_fusion
  172.4 0.2 select_reduce_fusion.1
  172.5 0.8 fusion.37
  173.3 0.6 maximum_maximum_fusion
  173.9 1.6 convolution_convert_fusion.1
  175.4 1.8 pad_maximum_fusion.1
  177.2 0.7 copy.23
  (18 shorter events, 0.4 us)
Async XLA Ops:
  0.6 4.6 %copy-start = (bf16[256,1024]{1,0:T(8,128)(2,1)S(1)}, bf16[256,1024]{1,0:T(8,128)(2,1)}, u32[]{:S(2)}) copy-start(bf16[256,1024]{1,0:T(8,128)(2,1)} %param.6) | copy-start | bytes 1572868
  5.2 1.0 copy-start.1
  171.1 6.1 %copy-start.2 = (bf16[3,64,768]{2,1,0:T(8,128)(2,1)S(1)}, bf16[3,64,768]{2,1,0:T(8,128)(2,1)}, u32[]{:S(2)}) copy-start(bf16[3,64,768]{2,1,0:T(8,128)(2,1)} %get-tuple-element.10) | copy-start | bytes 884740

commit v8 on v5

--- a/solution.py
+++ b/solution.py
@@ -65,8 +65,8 @@
     return jnp.concatenate([input_grad, tail], axis=1), grads
 
 
-def exchange_kernel(p0_ref, p1_ref, w_ref, ret0_ref, ret1_ref, out_ref,
-                    recv, back, grad_ref, round_a, round_b, first_a, first_b,
+def exchange_kernel(slot_ref, x_ref, qa_ref, qb_ref, w_ref, out_ref, tg_ref, gs_ref,
+                    p0, p1, ret0, ret1, recv, back, grad_ref, round_a, round_b, first_a, first_b,
                     part_a, part_b, second_a, second_b, send_sem, recv_sem, rs_send, rs_recv):
     n = lax.axis_size("expert")
     me = lax.axis_index("expert")
@@ -74,12 +74,42 @@
     row = lax.axis_index("dp")
     phases = recv.shape[0]
     splits = phases // MICRO
-    capacity = p0_ref.shape[0] // n
+    capacity = p0.shape[0] // n
+    batch_rows = x_ref.shape[0] // MICRO
     piece = capacity // splits
     width = w_ref.shape[1]
     part = out_ref.shape[1]
-    payloads = (p0_ref, p1_ref)
-    returns = (ret0_ref, ret1_ref)
+    payloads = (p0, p1)
+    returns = (ret0, ret1)
+
+    def selections(micro):
+        position = lax.broadcasted_iota(jnp.int32, (p0.shape[0], batch_rows), 0)
+        first = position == slot_ref[micro, 0:1, :]
+        second = position == slot_ref[micro, 1:2, :]
+        return first, second
+
+    def pack(micro):
+        first, second = selections(micro)
+        first_b = jnp.where(first, 1.0, 0.0).astype(BF16)
+        second_b = jnp.where(second, 1.0, 0.0).astype(BF16)
+        both_b = jnp.where(first | second, 1.0, 0.0).astype(BF16)
+        rows = pl.ds(micro * batch_rows, batch_rows)
+        dst = payloads[micro]
+        dst[:, :width] = mm(both_b, x_ref[rows, :]).astype(BF16)
+        dst[:, width:] = (mm(first_b, qa_ref[rows, :]) + mm(second_b, qb_ref[rows, :])).astype(BF16)
+
+    def unpack(micro):
+        first, second = selections(micro)
+        both_b = jnp.where(first | second, 1.0, 0.0).astype(BF16)
+        held = returns[micro][...]
+        rows = pl.ds(micro * batch_rows, batch_rows)
+        tg_ref[rows, :] = lax.dot_general(
+            both_b, held[:, :width], CONTRACT_FIRST, preferred_element_type=F32
+        ).astype(BF16)
+        gate_sum = held[:, width:width + 1].astype(F32) + held[:, width + 1:width + 2].astype(F32)
+        for index, chosen in enumerate((first, second)):
+            at = 2 * micro + index
+            gs_ref[at:at + 1, :] = jnp.sum(jnp.where(chosen, gate_sum, 0.0), axis=0, keepdims=True)
 
     barrier = pltpu.get_barrier_semaphore()
     for k in range(1, n):
@@ -88,6 +118,7 @@
     for k in range(1, n_row):
         peer = lax.rem(row + k, n_row)
         pl.semaphore_signal(barrier, inc=1, device_id=(peer, me), device_id_type=MESH)
+    pack(0)
     pl.semaphore_wait(barrier, n - 1 + n_row - 1)
 
     def slot_rows(expert, phase):
@@ -219,6 +250,7 @@
         out[:, width:] = tail.astype(BF16)
 
     send_forward(0)
+    pack(1)
     for phase in range(phases):
         wait_all(recv.at[phase], phase)
         if phase + 1 < phases:
@@ -226,10 +258,14 @@
         compute(phase)
         send_back(phase)
 
+    wait_all(back.at[0], phases)
+    unpack(0)
     reduce_grads()
 
     for phase in range(phases):
-        wait_all(back.at[phase], phases + phase)
+        if phase > 0:
+            wait_all(back.at[phase], phases + phase)
+            unpack(phase)
         wait_sent(recv.at[phase], phase)
         wait_sent(back.at[phase], phases + phase)
     rest = pl.ds(0, side - 1)
@@ -237,24 +273,33 @@
         pltpu.make_async_copy(buf.at[rest], buf.at[rest], rs_send.at[sem]).wait()
 
 
-def exchange(p0, p1, weights, n_row):
-    slots, full = p0.shape
+def exchange(slots, tokens, scaled_first, scaled_second, weights, n_row, capacity):
+    n_expert = lax.axis_size("expert")
+    rows = n_expert * capacity
     width = weights.shape[1]
+    full = 2 * width
     part = width // n_row
-    held = slots // SPLITS
-    back = jax.ShapeDtypeStruct((slots, width + PAD), BF16)
+    back = (rows, width + PAD)
     share = (weights.shape[0], part, weights.shape[2])
     quarter = (weights.shape[0], part, weights.shape[2] // 2)
-    phases = MICRO * SPLITS
+    phases = MICRO
     vmem = pl.BlockSpec(memory_space=pltpu.VMEM)
     return pl.pallas_call(
         exchange_kernel,
-        out_shape=(back, back, jax.ShapeDtypeStruct(share, BF16)),
-        in_specs=[vmem] * 3,
+        out_shape=(
+            jax.ShapeDtypeStruct(share, BF16),
+            jax.ShapeDtypeStruct(tokens.shape, BF16),
+            jax.ShapeDtypeStruct((2 * MICRO, tokens.shape[0] // MICRO), F32),
+        ),
+        in_specs=[vmem] * 5,
         out_specs=(vmem, vmem, vmem),
         scratch_shapes=[
-            pltpu.VMEM((phases, held, full), BF16),
-            pltpu.VMEM((phases, held, width + PAD), BF16),
+            pltpu.VMEM((rows, full), BF16),
+            pltpu.VMEM((rows, full), BF16),
+            pltpu.VMEM(back, BF16),
+            pltpu.VMEM(back, BF16),
+            pltpu.VMEM((phases, rows, full), BF16),
+            pltpu.VMEM((phases,) + back, BF16),
             pltpu.VMEM(weights.shape, F32),
             pltpu.VMEM((SIDE, SIDE) + quarter, BF16),
             pltpu.VMEM((SIDE, SIDE) + quarter, BF16),
@@ -272,7 +317,17 @@
         compiler_params=pltpu.CompilerParams(
             collective_id=0, has_side_effects=True, vmem_limit_bytes=62 * 1024 * 1024
         ),
-    )(p0, p1, weights)
+    )(slots, tokens, scaled_first, scaled_second, weights)
+
+
+def route_slot_rows(ids_block, expert_count, capacity):
+    flat_ids = ids_block.reshape(-1)
+    one_hot = (flat_ids[:, None] == jnp.arange(expert_count, dtype=jnp.int32)[None, :]).astype(
+        jnp.int32
+    )
+    earlier = jnp.cumsum(one_hot, axis=0) - one_hot
+    rank_slot = jnp.sum(earlier * one_hot, axis=1)
+    return (flat_ids * capacity + rank_slot).reshape(-1, 2).T
 
 
 def on_device(tokens, cotangent, gates, expert_ids, expert_weights):
@@ -280,47 +335,22 @@
     expert_count = n_expert * expert_weights.shape[0]
     batch_rows = tokens.shape[0] // MICRO
     capacity = max(2, 4 * batch_rows // expert_count)
-    width = tokens.shape[1]
-
-    masks, gate_list, payloads = [], [], []
-    for micro_index in range(MICRO):
-        lower = micro_index * batch_rows
-        upper = lower + batch_rows
-        first, second = route_masks(expert_ids[lower:upper], expert_count, capacity)
-        both = (first | second).astype(BF16)
-        cot = cotangent[lower:upper].astype(F32)
-        gate = gates[lower:upper].astype(F32)
-        scaled_first = (gate[:, 0:1] * cot).astype(BF16)
-        scaled_second = (gate[:, 1:2] * cot).astype(BF16)
-        rows_in = mm(both, tokens[lower:upper]).astype(BF16)
-        rows_scaled = (
-            mm(first.astype(BF16), scaled_first) + mm(second.astype(BF16), scaled_second)
-        ).astype(BF16)
-        payloads.append(jnp.concatenate([rows_in, rows_scaled], axis=1))
-        masks.append((first, second, both))
-        gate_list.append(gate)
-
-    ret0, ret1, weights_grad = exchange(
-        payloads[0], payloads[1], expert_weights[0], lax.axis_size("dp")
-    )
-
-    token_parts, gate_parts = [], []
-    for (first, second, both), gate, ret in zip(masks, gate_list, (ret0, ret1)):
-        token_grad = lax.dot_general(
-            both, ret[:, :width], CONTRACT_FIRST, preferred_element_type=F32
-        ).astype(BF16)
-        gate_sum = ret[:, width].astype(F32) + ret[:, width + 1].astype(F32)
-        sum_first = jnp.sum(jnp.where(first, gate_sum[:, None], 0.0), axis=0)
-        sum_second = jnp.sum(jnp.where(second, gate_sum[:, None], 0.0), axis=0)
-        gate_grad = jnp.stack([sum_first / gate[:, 0], sum_second / gate[:, 1]], axis=1)
-        token_parts.append(token_grad)
-        gate_parts.append(gate_grad.astype(BF16))
-
-    return (
-        jnp.concatenate(token_parts, axis=0),
-        jnp.concatenate(gate_parts, axis=0),
-        weights_grad[None],
-    )
+    slots = jnp.stack(
+        [
+            route_slot_rows(expert_ids[m * batch_rows:(m + 1) * batch_rows], expert_count, capacity)
+            for m in range(MICRO)
+        ]
+    )
+    cot = cotangent.astype(F32)
+    gate = gates.astype(F32)
+    scaled_first = (gate[:, 0:1] * cot).astype(BF16)
+    scaled_second = (gate[:, 1:2] * cot).astype(BF16)
+    weights_grad, token_grad, gate_sums = exchange(
+        slots, tokens, scaled_first, scaled_second, expert_weights[0],
+        lax.axis_size("dp"), capacity,
+    )
+    sums = gate_sums.reshape(MICRO, 2, batch_rows).transpose(0, 2, 1).reshape(-1, 2)
+    return token_grad, (sums / gate).astype(BF16), weights_grad[None]
 
 
 def solution(mesh):

time: 178 us -> 171 us (0.961)
  matrix products: 5.82 us -> 0 us
  local copies, waits for them, and re-layouts: 3.25 us -> 6.63 us
  other arithmetic: 9.45 us -> 6.23 us
    dot_general x8 -> x0, matrix products: 5.82 us -> none  [the longest x6 3.85 us: mm(): return jnp.dot(a, b, preferred_element_type=F32)]
    concatenate x4 -> x0, other arithmetic: 4.42 us -> none  [the longest x2 3.02 us: on_device(): payloads.append(jnp.concatenate([rows_in, rows_scaled], axis=1))]
    convert_element_type x3 -> x4, other arithmetic: 0.77 us -> 3.49 us  [the longest x1 2.23 us: on_device(): scaled_second = (gate[:, 1:2] * cot).astype(BF16)]
    unnamed x11 -> x4, local copies, waits for them, and re-layouts: 0.96 us -> 3.56 us
    add x4 -> x0, other arithmetic: 2.51 us -> none  [the longest x2 2.49 us: on_device(): gate_sum = ret[:, width].astype(F32) + ret[:, width + 1].astype(F32)]
where the time goes in v8:
time: 171 us
  Pallas kernels  157 us (92%)
  local copies, waits for them, and re-layouts  6.63 us (4%)
  other arithmetic  6.23 us (4%)
    pallas_call x1, Pallas kernels, exchange(): pl.pallas_call(exchange_kernel, out_shape=(jax.ShapeDtypeStruct(share, BF...  157 us
    unnamed x4, local copies, waits for them, and re-layouts  3.56 us

profile of v8, /device:TPU:65, one launch (start us, length us, event | category | flops | bytes accessed | tf_op | source)
XLA Modules:
  0.0 170.8 jit_solution(16210175066464200485)
XLA Ops:
  0.6 0.0 copy-start
  0.6 0.8 fusion.11
  1.4 0.7 fusion.10
  2.1 0.1 copy.9
  2.2 0.1 eq.54
  2.4 0.1 eq.50
  2.5 0.6 reduce-window.14
  3.1 0.2 slice_reduce_fusion.1
  3.3 0.1 fusion.7
  3.4 0.1 reduce_sum.23
  3.6 0.1 copy.12
  3.7 0.1 copy.13
  3.8 0.1 eq.62
  3.9 0.1 eq.58
  4.1 0.6 reduce-window.16
  4.7 0.2 slice_reduce_fusion
  4.9 0.1 fusion.4
  5.0 0.1 reduce_sum.25
  5.1 0.1 copy.16
  5.2 0.7 add_bitcast_fusion.3
  5.9 0.6 pad_add_fusion.slot_ref
  6.5 2.2 %fusion.1 = (bf16[256,1024]{1,0:T(8,128)(2,1)}, bf16[256,1024]{1,0:T(8,128)(2,1)}) fusion(bf16[256,1024]{1,0:T(8,128)(2,1)} %param.6, f32[256]{0:T(256)S(1)} %bitcast.57, f32[256]{0:T(256)S(1)} %bitcast.58), kind=kLoop, calls=%fused_computation.3 | loop fusion | flops 1310720 | bytes 1574912 | tf_op jit(solution)/shard_map/convert_element_type | solution.py:347
  8.7 157.3 %shard_map.76 = (bf16[3,64,768]{2,1,0:T(8,128)(2,1)}, bf16[256,1024]{1,0:T(8,128)(2,1)}, f32[4,128]{1,0:T(4,128)}) custom-call(s32[2,2,128]{2,1,0:T(2,128)} %pad_add_fusion.slot_ref, bf16[256,1024]{1,0:T(8,128)(2,1)} %x_ref.1, bf16[256,1024]{1,0:T(8,128)(2,1)} %get-tuple-element.10.qa_ref, bf16[256,1024]{1,0:T(8,128)(2,1)} %get-tuple-element.9.qb_ref, ...), custom_call_target="tpu_custom_call" | custom-call | tf_op jit(solution)/shard_map/pallas_call | solution.py:287
  166.0 0.0 copy-done
  166.0 1.2 divide_convert_fusion
  167.3 1.9 %copy.24 = bf16[256,1024]{1,0:T(8,128)(2,1)} copy(bf16[256,1024]{1,0:T(8,128)(2,1)} %get-tuple-element.20) | data formatting | bytes 1048576
  169.2 1.7 copy.25
  (6 shorter events, 0.1 us)
Async XLA Ops:
  0.6 165.4 %copy-start = (bf16[256,2]{0,1:T(2,128)(2,1)S(1)}, bf16[256,2]{0,1:T(2,128)(2,1)}, u32[]{:S(2)}) copy-start(bf16[256,2]{0,1:T(2,128)(2,1)} %param.7) | copy-start | bytes 3076

commit v9 on v8

--- a/solution.py
+++ b/solution.py
@@ -65,7 +65,7 @@
     return jnp.concatenate([input_grad, tail], axis=1), grads
 
 
-def exchange_kernel(slot_ref, x_ref, qa_ref, qb_ref, w_ref, out_ref, tg_ref, gs_ref,
+def exchange_kernel(slot_ref, x_ref, cot_ref, gate_ref, w_ref, out_ref, tg_ref, gs_ref,
                     p0, p1, ret0, ret1, recv, back, grad_ref, round_a, round_b, first_a, first_b,
                     part_a, part_b, second_a, second_b, send_sem, recv_sem, rs_send, rs_recv):
     n = lax.axis_size("expert")
@@ -96,7 +96,11 @@
         rows = pl.ds(micro * batch_rows, batch_rows)
         dst = payloads[micro]
         dst[:, :width] = mm(both_b, x_ref[rows, :]).astype(BF16)
-        dst[:, width:] = (mm(first_b, qa_ref[rows, :]) + mm(second_b, qb_ref[rows, :])).astype(BF16)
+        cot = cot_ref[rows, :].astype(F32)
+        gate = gate_ref[rows, :].astype(F32)
+        scaled_first = (gate[:, 0:1] * cot).astype(BF16)
+        scaled_second = (gate[:, 1:2] * cot).astype(BF16)
+        dst[:, width:] = (mm(first_b, scaled_first) + mm(second_b, scaled_second)).astype(BF16)
 
     def unpack(micro):
         first, second = selections(micro)
@@ -273,7 +277,7 @@
         pltpu.make_async_copy(buf.at[rest], buf.at[rest], rs_send.at[sem]).wait()
 
 
-def exchange(slots, tokens, scaled_first, scaled_second, weights, n_row, capacity):
+def exchange(slots, tokens, cotangent, gates, weights, n_row, capacity):
     n_expert = lax.axis_size("expert")
     rows = n_expert * capacity
     width = weights.shape[1]
@@ -317,7 +321,7 @@
         compiler_params=pltpu.CompilerParams(
             collective_id=0, has_side_effects=True, vmem_limit_bytes=62 * 1024 * 1024
         ),
-    )(slots, tokens, scaled_first, scaled_second, weights)
+    )(slots, tokens, cotangent, gates, weights)
 
 
 def route_slot_rows(ids_block, expert_count, capacity):
@@ -341,12 +345,9 @@
             for m in range(MICRO)
         ]
     )
-    cot = cotangent.astype(F32)
     gate = gates.astype(F32)
-    scaled_first = (gate[:, 0:1] * cot).astype(BF16)
-    scaled_second = (gate[:, 1:2] * cot).astype(BF16)
     weights_grad, token_grad, gate_sums = exchange(
-        slots, tokens, scaled_first, scaled_second, expert_weights[0],
+        slots, tokens, cotangent, gates, expert_weights[0],
         lax.axis_size("dp"), capacity,
     )
     sums = gate_sums.reshape(MICRO, 2, batch_rows).transpose(0, 2, 1).reshape(-1, 2)

time: 171 us -> 169 us (0.988)
  other arithmetic: 6.23 us -> 3.98 us
    convert_element_type x1 -> x0, other arithmetic: 2.23 us -> none  [on_device(): scaled_second = (gate[:, 1:2] * cot).astype(BF16)]
    unnamed x4 -> x5, local copies, waits for them, and re-layouts: 3.56 us -> 5 us
where the time goes in v9:
time: 169 us
  Pallas kernels  157 us (93%)
  local copies, waits for them, and re-layouts  7.28 us (4%)
  other arithmetic  3.98 us (2%)
    pallas_call x1, Pallas kernels, exchange(): pl.pallas_call(exchange_kernel, out_shape=(jax.ShapeDtypeStruct(share, BF...  157 us
    unnamed x5, local copies, waits for them, and re-layouts  5 us

profile of v9, /device:TPU:65, one launch (start us, length us, event | category | flops | bytes accessed | tf_op | source)
XLA Modules:
  0.0 169.1 jit_solution(716764536830502065)
XLA Ops:
  0.6 0.0 copy-start
  0.6 0.7 fusion.9
  1.3 0.1 copy.10
  1.5 0.1 eq.54
  1.6 0.1 eq.50
  1.8 0.6 reduce-window.14
  2.3 0.2 slice_reduce_fusion.1
  2.6 0.1 fusion.5
  2.7 0.1 reduce_sum.23
  2.8 0.1 copy.13
  2.9 0.1 copy.14
  3.0 0.1 eq.62
  3.2 0.1 eq.58
  3.3 0.6 reduce-window.16
  3.9 0.2 slice_reduce_fusion
  4.1 0.1 fusion.2
  4.2 0.1 reduce_sum.25
  4.4 0.1 copy.17
  4.4 0.7 add_bitcast_fusion.3
  5.2 0.6 pad_add_fusion.slot_ref
  5.7 1.4 copy.18.gate_ref
  7.2 157.1 %shard_map.76 = (bf16[3,64,768]{2,1,0:T(8,128)(2,1)}, bf16[256,1024]{1,0:T(8,128)(2,1)}, f32[4,128]{1,0:T(4,128)}) custom-call(s32[2,2,128]{2,1,0:T(2,128)} %pad_add_fusion.slot_ref, bf16[256,1024]{1,0:T(8,128)(2,1)} %x_ref.1, bf16[256,1024]{1,0:T(8,128)(2,1)} %cot_ref.1, bf16[256,2]{1,0:T(8,128)(2,1)} %copy.18.gate_ref, bf16[3,1024,768]{2,1,0:T(8,128)(2,1)} %bitcast.53), custom_call_target="tpu_custom_call" | custom-call | tf_op jit(solution)/shard_map/pallas_call | solution.py:291
  164.3 0.0 copy-done
  164.3 1.2 fusion.8
  165.5 1.9 %copy.26 = bf16[256,1024]{1,0:T(8,128)(2,1)} copy(bf16[256,1024]{1,0:T(8,128)(2,1)} %get-tuple-element.16) | data formatting | bytes 1048576
  167.4 1.7 %copy.27 = bf16[1,3,64,768]{3,2,1,0:T(8,128)(2,1)} copy(bf16[1,3,64,768]{3,2,1,0:T(8,128)(2,1)} %bitcast.54) | data formatting | bytes 589824
  (6 shorter events, 0.1 us)
Async XLA Ops:
  0.6 163.6 %copy-start = (bf16[256,2]{0,1:T(2,128)(2,1)S(1)}, bf16[256,2]{0,1:T(2,128)(2,1)}, u32[]{:S(2)}) copy-start(bf16[256,2]{0,1:T(2,128)(2,1)} %param.7) | copy-start | bytes 3076

commit v10 on v9

--- a/solution.py
+++ b/solution.py
@@ -65,7 +65,7 @@
     return jnp.concatenate([input_grad, tail], axis=1), grads
 
 
-def exchange_kernel(slot_ref, x_ref, cot_ref, gate_ref, w_ref, out_ref, tg_ref, gs_ref,
+def exchange_kernel(ids_ref, x_ref, cot_ref, gate_ref, w_ref, out_ref, tg_ref, gs_ref,
                     p0, p1, ret0, ret1, recv, back, grad_ref, round_a, round_b, first_a, first_b,
                     part_a, part_b, second_a, second_b, send_sem, recv_sem, rs_send, rs_recv):
     n = lax.axis_size("expert")
@@ -76,6 +76,7 @@
     splits = phases // MICRO
     capacity = p0.shape[0] // n
     batch_rows = x_ref.shape[0] // MICRO
+    n_experts = n * (p0.shape[0] // n // capacity)
     piece = capacity // splits
     width = w_ref.shape[1]
     part = out_ref.shape[1]
@@ -83,10 +84,20 @@
     returns = (ret0, ret1)
 
     def selections(micro):
-        position = lax.broadcasted_iota(jnp.int32, (p0.shape[0], batch_rows), 0)
-        first = position == slot_ref[micro, 0:1, :]
-        second = position == slot_ref[micro, 1:2, :]
-        return first, second
+        rows = pl.ds(micro * batch_rows, batch_rows)
+        ids = ids_ref[rows, :]
+        expert = lax.broadcasted_iota(jnp.int32, (batch_rows, n_experts), 1)
+        hot = [jnp.where(expert == ids[:, k:k + 1], 1.0, 0.0) for k in range(2)]
+        token = lax.broadcasted_iota(jnp.int32, (batch_rows, batch_rows), 0)
+        other = lax.broadcasted_iota(jnp.int32, (batch_rows, batch_rows), 1)
+        earlier = jnp.where(token > other, 1.0, 0.0).astype(BF16)
+        counts = mm(earlier, (hot[0] + hot[1]).astype(BF16))
+        position = lax.broadcasted_iota(jnp.int32, (batch_rows, p0.shape[0]), 1)
+        chosen = []
+        for k in range(2):
+            rank = jnp.sum(counts * hot[k], axis=1, keepdims=True).astype(jnp.int32)
+            chosen.append(position == ids[:, k:k + 1] * capacity + rank)
+        return chosen[0], chosen[1]
 
     def pack(micro):
         first, second = selections(micro)
@@ -95,25 +106,27 @@
         both_b = jnp.where(first | second, 1.0, 0.0).astype(BF16)
         rows = pl.ds(micro * batch_rows, batch_rows)
         dst = payloads[micro]
-        dst[:, :width] = mm(both_b, x_ref[rows, :]).astype(BF16)
         cot = cot_ref[rows, :].astype(F32)
         gate = gate_ref[rows, :].astype(F32)
         scaled_first = (gate[:, 0:1] * cot).astype(BF16)
         scaled_second = (gate[:, 1:2] * cot).astype(BF16)
-        dst[:, width:] = (mm(first_b, scaled_first) + mm(second_b, scaled_second)).astype(BF16)
+        dst[:, :width] = lax.dot_general(
+            both_b, x_ref[rows, :], CONTRACT_FIRST, preferred_element_type=F32
+        ).astype(BF16)
+        dst[:, width:] = (
+            lax.dot_general(first_b, scaled_first, CONTRACT_FIRST, preferred_element_type=F32)
+            + lax.dot_general(second_b, scaled_second, CONTRACT_FIRST, preferred_element_type=F32)
+        ).astype(BF16)
 
     def unpack(micro):
         first, second = selections(micro)
         both_b = jnp.where(first | second, 1.0, 0.0).astype(BF16)
         held = returns[micro][...]
         rows = pl.ds(micro * batch_rows, batch_rows)
-        tg_ref[rows, :] = lax.dot_general(
-            both_b, held[:, :width], CONTRACT_FIRST, preferred_element_type=F32
-        ).astype(BF16)
-        gate_sum = held[:, width:width + 1].astype(F32) + held[:, width + 1:width + 2].astype(F32)
+        tg_ref[rows, :] = mm(both_b, held[:, :width]).astype(BF16)
         for index, chosen in enumerate((first, second)):
-            at = 2 * micro + index
-            gs_ref[at:at + 1, :] = jnp.sum(jnp.where(chosen, gate_sum, 0.0), axis=0, keepdims=True)
+            picked = mm(jnp.where(chosen, 1.0, 0.0).astype(BF16), held[:, width:])
+            gs_ref[rows, index:index + 1] = picked[:, 0:1] + picked[:, 1:2]
 
     barrier = pltpu.get_barrier_semaphore()
     for k in range(1, n):
@@ -293,7 +306,7 @@
         out_shape=(
             jax.ShapeDtypeStruct(share, BF16),
             jax.ShapeDtypeStruct(tokens.shape, BF16),
-            jax.ShapeDtypeStruct((2 * MICRO, tokens.shape[0] // MICRO), F32),
+            jax.ShapeDtypeStruct((tokens.shape[0], 2), F32),
         ),
         in_specs=[vmem] * 5,
         out_specs=(vmem, vmem, vmem),
@@ -339,19 +352,12 @@
     expert_count = n_expert * expert_weights.shape[0]
     batch_rows = tokens.shape[0] // MICRO
     capacity = max(2, 4 * batch_rows // expert_count)
-    slots = jnp.stack(
-        [
-            route_slot_rows(expert_ids[m * batch_rows:(m + 1) * batch_rows], expert_count, capacity)
-            for m in range(MICRO)
-        ]
-    )
     gate = gates.astype(F32)
     weights_grad, token_grad, gate_sums = exchange(
-        slots, tokens, cotangent, gates, expert_weights[0],
+        expert_ids, tokens, cotangent, gates, expert_weights[0],
         lax.axis_size("dp"), capacity,
     )
-    sums = gate_sums.reshape(MICRO, 2, batch_rows).transpose(0, 2, 1).reshape(-1, 2)
-    return token_grad, (sums / gate).astype(BF16), weights_grad[None]
+    return token_grad, (gate_sums / gate).astype(BF16), weights_grad[None]
 
 
 def solution(mesh):

time: 169 us -> 168 us (level)
  other arithmetic: 3.98 us -> 0.93 us
    another operation x6 -> x0, other arithmetic: 2.56 us -> none  [the longest x2 1.3 us: on_device(): jnp.stack([route_slot_rows(expert_ids[m * batch_rows:(m + 1) * batch_rows...]
    unnamed x5, local copies, waits for them, and re-layouts: 5 us -> 7.13 us
where the time goes in v10:
time: 168 us; the launch traced here: 167 us
  Pallas kernels  158 us (94%)
  local copies, waits for them, and re-layouts  7.93 us (5%)
    pallas_call x1, Pallas kernels, exchange(): pl.pallas_call(exchange_kernel, out_shape=(jax.ShapeDtypeStruct(share, BF...  158 us
    unnamed x5, local copies, waits for them, and re-layouts  7.13 us

profile of v10, /device:TPU:65, one launch (start us, length us, event | category | flops | bytes accessed | tf_op | source)
XLA Modules:
  0.0 167.3 jit_solution(7861423416701262350)
XLA Ops:
  0.6 1.4 copy.9.gate_ref
  2.1 1.5 copy.8.ids_ref
  3.5 0.8 copy.10
  4.3 157.8 %shard_map.76 = (bf16[3,64,768]{2,1,0:T(8,128)(2,1)}, bf16[256,1024]{1,0:T(8,128)(2,1)}, f32[256,2]{1,0:T(8,128)}) custom-call(s32[256,2]{1,0:T(8,128)} %copy.8.ids_ref, bf16[256,1024]{1,0:T(8,128)(2,1)} %x_ref.1, bf16[256,1024]{1,0:T(8,128)(2,1)} %cot_ref.1, bf16[256,2]{1,0:T(8,128)(2,1)} %copy.9.gate_ref, bf16[3,1024,768]{2,1,0:T(8,128)(2,1)} %bitcast.2), custom_call_target="tpu_custom_call" | custom-call | tf_op jit(solution)/shard_map/pallas_call | solution.py:304
  162.2 0.9 divide_convert_fusion
  163.1 0.7 copy.11
  163.8 1.9 %copy.14 = bf16[256,1024]{1,0:T(8,128)(2,1)} copy(bf16[256,1024]{1,0:T(8,128)(2,1)} %get-tuple-element.15) | data formatting | bytes 1048576
  165.6 1.7 %copy.15 = bf16[1,3,64,768]{3,2,1,0:T(8,128)(2,1)} copy(bf16[1,3,64,768]{3,2,1,0:T(8,128)(2,1)} %bitcast.3) | data formatting | bytes 589824

commit v11 on v9

--- a/solution.py
+++ b/solution.py
@@ -65,7 +65,7 @@
     return jnp.concatenate([input_grad, tail], axis=1), grads
 
 
-def exchange_kernel(slot_ref, x_ref, cot_ref, gate_ref, w_ref, out_ref, tg_ref, gs_ref,
+def exchange_kernel(ids_ref, x_ref, cot_ref, gate_ref, w_ref, out_ref, tg_ref, gs_ref,
                     p0, p1, ret0, ret1, recv, back, grad_ref, round_a, round_b, first_a, first_b,
                     part_a, part_b, second_a, second_b, send_sem, recv_sem, rs_send, rs_recv):
     n = lax.axis_size("expert")
@@ -76,6 +76,7 @@
     splits = phases // MICRO
     capacity = p0.shape[0] // n
     batch_rows = x_ref.shape[0] // MICRO
+    n_experts = n * (p0.shape[0] // n // capacity)
     piece = capacity // splits
     width = w_ref.shape[1]
     part = out_ref.shape[1]
@@ -83,24 +84,30 @@
     returns = (ret0, ret1)
 
     def selections(micro):
+        rows = pl.ds(micro * batch_rows, batch_rows)
+        ids = ids_ref[:, rows]
+        expert = lax.broadcasted_iota(jnp.int32, (n_experts, batch_rows), 0)
+        hot = [jnp.where(expert == ids[k:k + 1, :], 1.0, 0.0) for k in range(2)]
+        before = lax.broadcasted_iota(jnp.int32, (batch_rows, batch_rows), 0)
+        after = lax.broadcasted_iota(jnp.int32, (batch_rows, batch_rows), 1)
+        earlier = jnp.where(before < after, 1.0, 0.0).astype(BF16)
+        counts = mm((hot[0] + hot[1]).astype(BF16), earlier)
         position = lax.broadcasted_iota(jnp.int32, (p0.shape[0], batch_rows), 0)
-        first = position == slot_ref[micro, 0:1, :]
-        second = position == slot_ref[micro, 1:2, :]
-        return first, second
+        chosen = []
+        for k in range(2):
+            rank = jnp.sum(counts * hot[k], axis=0, keepdims=True).astype(jnp.int32)
+            chosen.append(position == ids[k:k + 1, :] * capacity + rank)
+        return chosen[0], chosen[1]
 
     def pack(micro):
         first, second = selections(micro)
-        first_b = jnp.where(first, 1.0, 0.0).astype(BF16)
-        second_b = jnp.where(second, 1.0, 0.0).astype(BF16)
+        rows = pl.ds(micro * batch_rows, batch_rows)
+        gate = gate_ref[:, rows].astype(F32)
         both_b = jnp.where(first | second, 1.0, 0.0).astype(BF16)
-        rows = pl.ds(micro * batch_rows, batch_rows)
+        gated = jnp.where(first, gate[0:1, :], jnp.where(second, gate[1:2, :], 0.0)).astype(BF16)
         dst = payloads[micro]
         dst[:, :width] = mm(both_b, x_ref[rows, :]).astype(BF16)
-        cot = cot_ref[rows, :].astype(F32)
-        gate = gate_ref[rows, :].astype(F32)
-        scaled_first = (gate[:, 0:1] * cot).astype(BF16)
-        scaled_second = (gate[:, 1:2] * cot).astype(BF16)
-        dst[:, width:] = (mm(first_b, scaled_first) + mm(second_b, scaled_second)).astype(BF16)
+        dst[:, width:] = mm(gated, cot_ref[rows, :]).astype(BF16)
 
     def unpack(micro):
         first, second = selections(micro)
@@ -112,8 +119,9 @@
         ).astype(BF16)
         gate_sum = held[:, width:width + 1].astype(F32) + held[:, width + 1:width + 2].astype(F32)
         for index, chosen in enumerate((first, second)):
-            at = 2 * micro + index
-            gs_ref[at:at + 1, :] = jnp.sum(jnp.where(chosen, gate_sum, 0.0), axis=0, keepdims=True)
+            gs_ref[index:index + 1, rows] = jnp.sum(
+                jnp.where(chosen, gate_sum, 0.0), axis=0, keepdims=True
+            )
 
     barrier = pltpu.get_barrier_semaphore()
     for k in range(1, n):
@@ -293,7 +301,7 @@
         out_shape=(
             jax.ShapeDtypeStruct(share, BF16),
             jax.ShapeDtypeStruct(tokens.shape, BF16),
-            jax.ShapeDtypeStruct((2 * MICRO, tokens.shape[0] // MICRO), F32),
+            jax.ShapeDtypeStruct((2, tokens.shape[0]), F32),
         ),
         in_specs=[vmem] * 5,
         out_specs=(vmem, vmem, vmem),
@@ -339,19 +347,12 @@
     expert_count = n_expert * expert_weights.shape[0]
     batch_rows = tokens.shape[0] // MICRO
     capacity = max(2, 4 * batch_rows // expert_count)
-    slots = jnp.stack(
-        [
-            route_slot_rows(expert_ids[m * batch_rows:(m + 1) * batch_rows], expert_count, capacity)
-            for m in range(MICRO)
-        ]
-    )
-    gate = gates.astype(F32)
+    gate = gates.T.astype(F32)
     weights_grad, token_grad, gate_sums = exchange(
-        slots, tokens, cotangent, gates, expert_weights[0],
+        expert_ids.T, tokens, cotangent, gates.T, expert_weights[0],
         lax.axis_size("dp"), capacity,
     )
-    sums = gate_sums.reshape(MICRO, 2, batch_rows).transpose(0, 2, 1).reshape(-1, 2)
-    return token_grad, (sums / gate).astype(BF16), weights_grad[None]
+    return token_grad, (gate_sums / gate).astype(BF16).T, weights_grad[None]
 
 
 def solution(mesh):

time: 169 us -> 163 us (0.964)
  local copies, waits for them, and re-layouts: 7.28 us -> 3.56 us
  other arithmetic: 3.98 us -> 1.24 us
    another operation x6 -> x0, other arithmetic: 2.56 us -> none  [the longest x2 1.3 us: on_device(): jnp.stack([route_slot_rows(expert_ids[m * batch_rows:(m + 1) * batch_rows...]
    unnamed x5 -> x4, local copies, waits for them, and re-layouts: 5 us -> 3.56 us
where the time goes in v11:
time: 163 us
  Pallas kernels  157 us (96%)
  local copies, waits for them, and re-layouts  3.56 us (2%)
    pallas_call x1, Pallas kernels, exchange(): pl.pallas_call(exchange_kernel, out_shape=(jax.ShapeDtypeStruct(share, BF...  157 us
    unnamed x4, local copies, waits for them, and re-layouts  3.56 us

profile of v11, /device:TPU:65, one launch (start us, length us, event | category | flops | bytes accessed | tf_op | source)
XLA Modules:
  0.0 162.8 jit_solution(16017606648202839211)
XLA Ops:
  0.6 0.0 copy-start
  0.6 157.4 %shard_map.76 = (bf16[3,64,768]{2,1,0:T(8,128)(2,1)}, bf16[256,1024]{1,0:T(8,128)(2,1)}, f32[2,256]{1,0:T(2,128)}) custom-call(s32[2,256]{1,0:T(2,128)} %bitcast.10, bf16[256,1024]{1,0:T(8,128)(2,1)} %x_ref.1, bf16[256,1024]{1,0:T(8,128)(2,1)} %cot_ref.1, bf16[2,256]{1,0:T(2,128)(2,1)} %bitcast.9, bf16[3,1024,768]{2,1,0:T(8,128)(2,1)} %bitcast.7), custom_call_target="tpu_custom_call" | custom-call | tf_op jit(solution)/shard_map/pallas_call | solution.py:299
  158.0 0.0 copy-done
  158.0 1.2 fusion.1
  159.3 1.9 %copy.10 = bf16[256,1024]{1,0:T(8,128)(2,1)} copy(bf16[256,1024]{1,0:T(8,128)(2,1)} %get-tuple-element.12) | data formatting | bytes 1048576
  161.2 1.7 %copy.11 = bf16[1,3,64,768]{3,2,1,0:T(8,128)(2,1)} copy(bf16[1,3,64,768]{3,2,1,0:T(8,128)(2,1)} %bitcast.8) | data formatting | bytes 589824
Async XLA Ops:
  0.6 157.4 %copy-start = (bf16[256,2]{0,1:T(2,128)(2,1)S(1)}, bf16[256,2]{0,1:T(2,128)(2,1)}, u32[]{:S(2)}) copy-start(bf16[256,2]{0,1:T(2,128)(2,1)} %param.7) | copy-start | bytes 3076

commit v12 on v11

--- a/solution.py
+++ b/solution.py
@@ -65,8 +65,8 @@
     return jnp.concatenate([input_grad, tail], axis=1), grads
 
 
-def exchange_kernel(ids_ref, x_ref, cot_ref, gate_ref, w_ref, out_ref, tg_ref, gs_ref,
-                    p0, p1, ret0, ret1, recv, back, grad_ref, round_a, round_b, first_a, first_b,
+def exchange_kernel(ids_ref, x_ref, cot_ref, gate_ref, w_ref, out_ref, tg_ref, gg_ref,
+                    gs_ref, p0, p1, ret0, ret1, recv, back, grad_ref, round_a, round_b, first_a, first_b,
                     part_a, part_b, second_a, second_b, send_sem, recv_sem, rs_send, rs_recv):
     n = lax.axis_size("expert")
     me = lax.axis_index("expert")
@@ -280,6 +280,7 @@
             unpack(phase)
         wait_sent(recv.at[phase], phase)
         wait_sent(back.at[phase], phases + phase)
+    gg_ref[...] = (gs_ref[...] / gate_ref[...].astype(F32)).astype(BF16)
     rest = pl.ds(0, side - 1)
     for sem, buf in enumerate((first_a, first_b, second_a, second_b)):
         pltpu.make_async_copy(buf.at[rest], buf.at[rest], rs_send.at[sem]).wait()
@@ -301,11 +302,12 @@
         out_shape=(
             jax.ShapeDtypeStruct(share, BF16),
             jax.ShapeDtypeStruct(tokens.shape, BF16),
-            jax.ShapeDtypeStruct((2, tokens.shape[0]), F32),
+            jax.ShapeDtypeStruct((2, tokens.shape[0]), BF16),
         ),
         in_specs=[vmem] * 5,
         out_specs=(vmem, vmem, vmem),
         scratch_shapes=[
+            pltpu.VMEM((2, tokens.shape[0]), F32),
             pltpu.VMEM((rows, full), BF16),
             pltpu.VMEM((rows, full), BF16),
             pltpu.VMEM(back, BF16),
@@ -347,12 +349,11 @@
     expert_count = n_expert * expert_weights.shape[0]
     batch_rows = tokens.shape[0] // MICRO
     capacity = max(2, 4 * batch_rows // expert_count)
-    gate = gates.T.astype(F32)
-    weights_grad, token_grad, gate_sums = exchange(
+    weights_grad, token_grad, gate_grad = exchange(
         expert_ids.T, tokens, cotangent, gates.T, expert_weights[0],
         lax.axis_size("dp"), capacity,
     )
-    return token_grad, (gate_sums / gate).astype(BF16).T, weights_grad[None]
+    return token_grad, gate_grad.T, weights_grad[None]
 
 
 def solution(mesh):

time: 163 us -> 163 us (level)
    unnamed x4 -> x3, local copies, waits for them, and re-layouts: 3.56 us -> 4.79 us
where the time goes in v12:
time: 163 us
  Pallas kernels  157 us (96%)
  local copies, waits for them, and re-layouts  4.79 us (3%)
    pallas_call x1, Pallas kernels, exchange(): pl.pallas_call(exchange_kernel, out_shape=(jax.ShapeDtypeStruct(share, BF...  157 us
    unnamed x3, local copies, waits for them, and re-layouts  4.79 us

profile of v12, /device:TPU:65, one launch (start us, length us, event | category | flops | bytes accessed | tf_op | source)
XLA Modules:
  0.0 162.8 jit_solution(17378273847969573331)
XLA Ops:
  0.6 157.4 %shard_map.76 = (bf16[3,64,768]{2,1,0:T(8,128)(2,1)}, bf16[256,1024]{1,0:T(8,128)(2,1)}, bf16[2,256]{1,0:T(2,128)(2,1)}) custom-call(s32[2,256]{1,0:T(2,128)} %bitcast.7, bf16[256,1024]{1,0:T(8,128)(2,1)} %x_ref.1, bf16[256,1024]{1,0:T(8,128)(2,1)} %cot_ref.1, bf16[2,256]{1,0:T(2,128)(2,1)} %bitcast.8, bf16[3,1024,768]{2,1,0:T(8,128)(2,1)} %bitcast.5), custom_call_target="tpu_custom_call" | custom-call | tf_op jit(solution)/shard_map/pallas_call | solution.py:300
  158.0 1.9 %copy.11 = bf16[256,1024]{1,0:T(8,128)(2,1)} copy(bf16[256,1024]{1,0:T(8,128)(2,1)} %get-tuple-element.12) | data formatting | bytes 1048576
  159.9 1.2 copy.12
  161.1 1.7 %copy.13 = bf16[1,3,64,768]{3,2,1,0:T(8,128)(2,1)} copy(bf16[1,3,64,768]{3,2,1,0:T(8,128)(2,1)} %bitcast.6) | data formatting | bytes 589824

commit v13 on v11

--- a/solution.py
+++ b/solution.py
@@ -142,7 +142,7 @@
 
     def scatter(phase, src_rows, dst_rows, src, dst, sem):
         pltpu.make_async_copy(src.at[src_rows(me)], dst.at[dst_rows(me)], recv_sem.at[sem]).start()
-        for k in range(1, n):
+        for k in sorted(range(1, n), key=lambda k: -min(k, n - k)):
             peer = lax.rem(me + k, n)
             pltpu.make_async_remote_copy(
                 src_ref=src.at[src_rows(peer)],

time: 163 us -> 164 us (level)
  no operation moved by 1% of the time
where the time goes in v13:
time: 164 us; the launch traced here: 163 us
  Pallas kernels  157 us (96%)
  local copies, waits for them, and re-layouts  3.56 us (2%)
    pallas_call x1, Pallas kernels, exchange(): pl.pallas_call(exchange_kernel, out_shape=(jax.ShapeDtypeStruct(share, BF...  157 us
    unnamed x4, local copies, waits for them, and re-layouts  3.56 us

profile of v13, /device:TPU:65, one launch (start us, length us, event | category | flops | bytes accessed | tf_op | source)
XLA Modules:
  0.0 162.8 jit_solution(3210543230825225111)
XLA Ops:
  0.6 0.0 copy-start
  0.6 157.3 %shard_map.76 = (bf16[3,64,768]{2,1,0:T(8,128)(2,1)}, bf16[256,1024]{1,0:T(8,128)(2,1)}, f32[2,256]{1,0:T(2,128)}) custom-call(s32[2,256]{1,0:T(2,128)} %bitcast.10, bf16[256,1024]{1,0:T(8,128)(2,1)} %x_ref.1, bf16[256,1024]{1,0:T(8,128)(2,1)} %cot_ref.1, bf16[2,256]{1,0:T(2,128)(2,1)} %bitcast.9, bf16[3,1024,768]{2,1,0:T(8,128)(2,1)} %bitcast.7), custom_call_target="tpu_custom_call" | custom-call | tf_op jit(solution)/shard_map/pallas_call | solution.py:299
  158.0 0.0 copy-done
  158.0 1.2 fusion.1
  159.2 1.9 %copy.10 = bf16[256,1024]{1,0:T(8,128)(2,1)} copy(bf16[256,1024]{1,0:T(8,128)(2,1)} %get-tuple-element.12) | data formatting | bytes 1048576
  161.1 1.7 %copy.11 = bf16[1,3,64,768]{3,2,1,0:T(8,128)(2,1)} copy(bf16[1,3,64,768]{3,2,1,0:T(8,128)(2,1)} %bitcast.8) | data formatting | bytes 589824
Async XLA Ops:
  0.6 157.4 %copy-start = (bf16[256,2]{0,1:T(2,128)(2,1)S(1)}, bf16[256,2]{0,1:T(2,128)(2,1)}, u32[]{:S(2)}) copy-start(bf16[256,2]{0,1:T(2,128)(2,1)} %param.7) | copy-start | bytes 3076

commit v14 on v11

--- a/solution.py
+++ b/solution.py
@@ -65,8 +65,8 @@
     return jnp.concatenate([input_grad, tail], axis=1), grads
 
 
-def exchange_kernel(ids_ref, x_ref, cot_ref, gate_ref, w_ref, out_ref, tg_ref, gs_ref,
-                    p0, p1, ret0, ret1, recv, back, grad_ref, round_a, round_b, first_a, first_b,
+def exchange_kernel(ids_ref, x_ref, cot_ref, gate_ref, w_ref, out_hbm, tg_hbm, gs_ref,
+                    out_ref, tg_ref, out_sem, p0, p1, ret0, ret1, recv, back, grad_ref, round_a, round_b, first_a, first_b,
                     part_a, part_b, second_a, second_b, send_sem, recv_sem, rs_send, rs_recv):
     n = lax.axis_size("expert")
     me = lax.axis_index("expert")
@@ -280,9 +280,17 @@
             unpack(phase)
         wait_sent(recv.at[phase], phase)
         wait_sent(back.at[phase], phases + phase)
+    results = [
+        pltpu.make_async_copy(src, dst, out_sem.at[index])
+        for index, (src, dst) in enumerate(((out_ref, out_hbm), (tg_ref, tg_hbm)))
+    ]
+    for copy in results:
+        copy.start()
     rest = pl.ds(0, side - 1)
     for sem, buf in enumerate((first_a, first_b, second_a, second_b)):
         pltpu.make_async_copy(buf.at[rest], buf.at[rest], rs_send.at[sem]).wait()
+    for copy in results:
+        copy.wait()
 
 
 def exchange(slots, tokens, cotangent, gates, weights, n_row, capacity):
@@ -304,8 +312,15 @@
             jax.ShapeDtypeStruct((2, tokens.shape[0]), F32),
         ),
         in_specs=[vmem] * 5,
-        out_specs=(vmem, vmem, vmem),
+        out_specs=(
+            pl.BlockSpec(memory_space=pl.ANY),
+            pl.BlockSpec(memory_space=pl.ANY),
+            vmem,
+        ),
         scratch_shapes=[
+            pltpu.VMEM(share, BF16),
+            pltpu.VMEM(tokens.shape, BF16),
+            pltpu.SemaphoreType.DMA((2,)),
             pltpu.VMEM((rows, full), BF16),
             pltpu.VMEM((rows, full), BF16),
             pltpu.VMEM(back, BF16),

time: 163 us -> 164 us (level)
  no operation moved by 1% of the time
where the time goes in v14:
time: 164 us; the launch traced here: 163 us
  Pallas kernels  158 us (96%)
  local copies, waits for them, and re-layouts  3.56 us (2%)
    pallas_call x1, Pallas kernels, exchange(): pl.pallas_call(exchange_kernel, out_shape=(jax.ShapeDtypeStruct(share, BF...  158 us
    unnamed x4, local copies, waits for them, and re-layouts  3.56 us

profile of v14, /device:TPU:65, one launch (start us, length us, event | category | flops | bytes accessed | tf_op | source)
XLA Modules:
  0.0 163.4 jit_solution(2185327990855018182)
XLA Ops:
  0.6 0.0 copy-start
  0.6 157.9 %shard_map.76 = (bf16[3,64,768]{2,1,0:T(8,128)(2,1)}, bf16[256,1024]{1,0:T(8,128)(2,1)}, f32[2,256]{1,0:T(2,128)}) custom-call(s32[2,256]{1,0:T(2,128)} %bitcast.10, bf16[256,1024]{1,0:T(8,128)(2,1)} %x_ref.1, bf16[256,1024]{1,0:T(8,128)(2,1)} %cot_ref.1, bf16[2,256]{1,0:T(2,128)(2,1)} %bitcast.9, bf16[3,1024,768]{2,1,0:T(8,128)(2,1)} %bitcast.7), custom_call_target="tpu_custom_call" | custom-call | tf_op jit(solution)/shard_map/pallas_call | solution.py:307
  158.6 0.0 copy-done
  158.6 1.2 fusion.1
  159.8 1.9 %copy.10 = bf16[256,1024]{1,0:T(8,128)(2,1)} copy(bf16[256,1024]{1,0:T(8,128)(2,1)} %get-tuple-element.12) | data formatting | bytes 1048576
  161.7 1.7 %copy.11 = bf16[1,3,64,768]{3,2,1,0:T(8,128)(2,1)} copy(bf16[1,3,64,768]{3,2,1,0:T(8,128)(2,1)} %bitcast.8) | data formatting | bytes 589824
Async XLA Ops:
  0.6 158.0 %copy-start = (bf16[256,2]{0,1:T(2,128)(2,1)S(1)}, bf16[256,2]{0,1:T(2,128)(2,1)}, u32[]{:S(2)}) copy-start(bf16[256,2]{0,1:T(2,128)(2,1)} %param.7) | copy-start | bytes 3076

commit v15 on v11

--- a/solution.py
+++ b/solution.py
@@ -245,10 +245,17 @@
         for index, value in enumerate(grads):
             if phase == 0:
                 grad_ref[index] = value
+            elif phase < phases - 1:
+                grad_ref[index] += value
             else:
-                grad_ref[index] += value
+                total = grad_ref[index] + value
+                for block in range(n_row):
+                    rounded = total[block * part:(block + 1) * part, :].astype(BF16)
+                    round_a[block % side, block // side, index] = rounded[:, :half]
+                    round_b[block // side, block % side, index] = rounded[:, half:]
         if phase == phases - 1:
-            scatter_grads()
+            spread(round_a, first_a, col_a, x_peer, 0)
+            spread(round_b, first_b, col_b, y_peer, 1)
         input_grad = (
             lax.dot_general(grad_pre_gate, w_gate, CONTRACT_LAST, preferred_element_type=F32)
             + lax.dot_general(grad_pre_up, w_up, CONTRACT_LAST, preferred_element_type=F32)

time: 163 us -> 163 us (level)
  no operation moved by 1% of the time
where the time goes in v15:
time: 163 us
  Pallas kernels  157 us (96%)
  local copies, waits for them, and re-layouts  3.56 us (2%)
    pallas_call x1, Pallas kernels, exchange(): pl.pallas_call(exchange_kernel, out_shape=(jax.ShapeDtypeStruct(share, BF...  157 us
    unnamed x4, local copies, waits for them, and re-layouts  3.56 us

profile of v15, /device:TPU:65, one launch (start us, length us, event | category | flops | bytes accessed | tf_op | source)
XLA Modules:
  0.0 162.8 jit_solution(6596247158277077485)
XLA Ops:
  0.6 0.0 copy-start
  0.6 157.4 %shard_map.76 = (bf16[3,64,768]{2,1,0:T(8,128)(2,1)}, bf16[256,1024]{1,0:T(8,128)(2,1)}, f32[2,256]{1,0:T(2,128)}) custom-call(s32[2,256]{1,0:T(2,128)} %bitcast.10, bf16[256,1024]{1,0:T(8,128)(2,1)} %x_ref.1, bf16[256,1024]{1,0:T(8,128)(2,1)} %cot_ref.1, bf16[2,256]{1,0:T(2,128)(2,1)} %bitcast.9, bf16[3,1024,768]{2,1,0:T(8,128)(2,1)} %bitcast.7), custom_call_target="tpu_custom_call" | custom-call | tf_op jit(solution)/shard_map/pallas_call | solution.py:306
  158.0 0.0 copy-done
  158.0 1.2 fusion.1
  159.3 1.9 %copy.10 = bf16[256,1024]{1,0:T(8,128)(2,1)} copy(bf16[256,1024]{1,0:T(8,128)(2,1)} %get-tuple-element.12) | data formatting | bytes 1048576
  161.2 1.7 %copy.11 = bf16[1,3,64,768]{3,2,1,0:T(8,128)(2,1)} copy(bf16[1,3,64,768]{3,2,1,0:T(8,128)(2,1)} %bitcast.8) | data formatting | bytes 589824
Async XLA Ops:
  0.6 157.4 %copy-start = (bf16[256,2]{0,1:T(2,128)(2,1)S(1)}, bf16[256,2]{0,1:T(2,128)(2,1)}, u32[]{:S(2)}) copy-start(bf16[256,2]{0,1:T(2,128)(2,1)} %param.7) | copy-start | bytes 3076
